TPU v7x, 32 devices: a whole 2x2x4 slice. The times are simulated.
32 devices in a mesh: pp: 4 (over y, x), cp: 4 (over z), tp: 2 (over core).
Axes of the slice: x: 2, y: 2, z: 4, core: 2. Of those that a mesh axis runs over, the one named last changes fastest.
Arguments:
- queries: bfloat16 [2048, 16384], P(('pp', 'cp'), 'tp'), may hold values from -12 to 12
- keys: bfloat16 [2048, 1024], P(('pp', 'cp'), 'tp'), may hold values from -12 to 12
- values: bfloat16 [2048, 1024], P(('pp', 'cp'), 'tp'), may hold values from -6 to 6
- pair_order: int32 [4, 4], replicated, may hold values from 0 to 3, each once within a row
- lengths: int32 [4, 2], replicated, may hold values from 128 to 256
- routes: int32 [4, 512, 1], P(None, 'cp'), may hold values from 0 to 7; in each aligned block of 128 rows (0 to 127, 128 to 255, ..., all dimensions but the last counted through in order) at most 32 rows name the same one
Outputs:
- rebalanced: bfloat16 [4096, 16384], P(('pp', 'cp', 'tp'))
Inputs may be any that keep to these rules, and one draw needn't show every extreme that they name: `routes`: at most 32 rows of one device's block name the same destination, and in some block one destination is named by exactly 32 rows.
All inputs are finite; a program needn't handle non-finite values.
Results may differ from a plain program's by a relative error of at most 0.003.
Values may be sent and summed in bfloat16 or wider, within the bound.
No kernel may reach another device: no remote copies, remote signals or barrier semaphores. Data moves between devices by JAX's collectives and lax.ppermute only.
A program may use at most 64 MiB of HBM per device.

v0:
```python
import jax
import jax.numpy as jnp
from jax import lax
from jax.experimental import pallas as pl
from jax.experimental.pallas import tpu as pltpu
from jax.sharding import PartitionSpec as P

HD = 128


masked_score = -1e30


def shifted(block, axis, distance):
    devices = range(lax.axis_size(axis))
    route = [((i - distance) % len(devices), i) for i in devices]
    return lax.ppermute(block, axis, route)


def pair_positions(pair_ids, block_len, cycle_size):
    offsets = jnp.arange(block_len, dtype=jnp.int32)
    first_half = pair_ids[:, None] * block_len + offsets[None, :]
    second_half = (2 * cycle_size - 1 - pair_ids)[:, None] * block_len + offsets[None, :]
    return jnp.concatenate([first_half, second_half], axis=1)


def dispatch_rows(attended, targets, dest_count, capacity):
    row_count = attended.shape[0]
    matches = targets[:, None] == jnp.arange(dest_count, dtype=jnp.int32)[None, :]
    row_ids = jnp.arange(row_count, dtype=jnp.int32)
    earlier = (row_ids[None, :] < row_ids[:, None]).astype(jnp.bfloat16)
    before = jnp.dot(earlier, matches.astype(jnp.bfloat16), preferred_element_type=jnp.float32)
    slot_index = jnp.sum(jnp.where(matches, before, 0.0), axis=1).astype(jnp.int32)
    slot_ids = jnp.arange(capacity, dtype=jnp.int32)
    picked_rows = jnp.logical_and(
        jnp.transpose(matches)[:, None, :], slot_index[None, None, :] == slot_ids[None, :, None]
    )
    selector = picked_rows.astype(jnp.bfloat16).reshape(dest_count * capacity, row_count)
    return jnp.dot(selector, attended, preferred_element_type=jnp.float32).astype(jnp.bfloat16)


def spread_rows(buffer, cycle_size, split_size, capacity, width):
    flat_buffer = buffer.reshape(cycle_size * split_size, capacity, width)
    moved = lax.all_to_all(flat_buffer, ("cp", "tp"), split_axis=0, concat_axis=0, tiled=True)
    moved = jnp.transpose(moved.reshape(cycle_size, split_size, capacity, width), (0, 2, 1, 3))
    return moved.reshape(cycle_size * capacity, split_size * width)


def arrange_rows(attended, routes, source, cycle_size, split_size):
    row_count, width = attended.shape
    dest_count = cycle_size * split_size
    capacity = 2 * row_count // dest_count
    targets = lax.dynamic_index_in_dim(routes, source, 0, keepdims=False)[:, 0]
    buffer = dispatch_rows(attended, targets, dest_count, capacity)
    buffer = buffer.reshape(cycle_size, split_size, capacity, width)
    return spread_rows(buffer, cycle_size, split_size, capacity, width)


def general_body(queries, keys, values, pair_order, lengths, routes):
    cycle_size = lax.axis_size("cp")
    split_size = lax.axis_size("tp")
    section = lax.axis_index("pp")
    place = lax.axis_index("cp")
    row_count = queries.shape[0]
    block_len = row_count // 4
    width = queries.shape[1]
    group_count = keys.shape[1] // HD
    group_size = width // keys.shape[1]
    score_scale = HD ** (-0.5)
    order_row = lax.dynamic_index_in_dim(pair_order, section, 0, keepdims=False)
    own_pair = lax.dynamic_index_in_dim(order_row, place, 0, keepdims=True)
    query_pos = pair_positions(own_pair, block_len, cycle_size).reshape(2 * block_len)
    limits = lax.dynamic_index_in_dim(lengths, section, 0, keepdims=False)
    query_rows = queries.reshape(2, 2 * block_len, group_count, group_size, HD)
    stat_shape = (2, 2 * block_len, group_count, group_size)
    start_state = (
        jnp.full(stat_shape, masked_score, jnp.float32),
        jnp.zeros(stat_shape, jnp.float32),
        jnp.zeros(stat_shape + (HD,), jnp.float32),
    )
    state = start_state
    key_piece = lax.all_gather(keys, "cp", axis=0, tiled=True)
    value_piece = lax.all_gather(values, "cp", axis=0, tiled=True)
    shard_count = key_piece.shape[0] // row_count
    first_shard = jnp.int32(0) // row_count
    for base in range(0, shard_count, 4):
        block = min(4, shard_count - base)
        key_block = key_piece[base * row_count : (base + block) * row_count].reshape(
            block, 2, 2 * block_len, group_count, HD
        )
        value_block = value_piece[base * row_count : (base + block) * row_count].reshape(
            block, 2, 2 * block_len, group_count, HD
        )
        shard_ids = first_shard + base + jnp.arange(block, dtype=jnp.int32)
        key_pos = pair_positions(order_row[shard_ids], block_len, cycle_size).reshape(
            block * 2 * block_len
        )
        allowed = jnp.logical_and(
            key_pos[None, None, :] <= query_pos[None, :, None],
            key_pos[None, None, :] < limits[:, None, None],
        )
        allowed = allowed[:, :, None, None, :]
        scores = jnp.einsum(
            "sqgrd,nskgd->sqgrnk", query_rows, key_block, preferred_element_type=jnp.float32
        )
        scores = scores.reshape(stat_shape + (block * 2 * block_len,)) * score_scale
        running_max, running_total, running_sum = state
        block_max = jnp.max(jnp.where(allowed, scores, masked_score), axis=4)
        new_max = jnp.maximum(running_max, block_max)
        weights = jnp.where(allowed, jnp.exp(scores - new_max[..., None]), 0.0)
        carry_factor = jnp.exp(running_max - new_max)
        running_total = running_total * carry_factor + jnp.sum(weights, axis=4)
        shaped = weights.astype(jnp.bfloat16).reshape(stat_shape + (block, 2 * block_len))
        running_sum = running_sum * carry_factor[..., None] + jnp.einsum(
            "sqgrnk,nskgd->sqgrd", shaped, value_block, preferred_element_type=jnp.float32
        )
        state = (new_max, running_total, running_sum)
    attended = (state[2] / state[1][..., None]).astype(jnp.bfloat16).reshape(row_count, width)
    arranged = arrange_rows(attended, routes, section, cycle_size, split_size)
    return shifted(arranged, "pp", 1)


def to_partner(block, mask):
    size = lax.axis_size("cp")
    return lax.ppermute(block, "cp", [(i, i ^ mask) for i in range(size)])


def to_next_section(block, mask):
    sections, size = lax.axis_size("pp"), lax.axis_size("cp")
    route = [
        (p * size + i, ((p + 1) % sections) * size + (i ^ mask))
        for p in range(sections)
        for i in range(size)
    ]
    return lax.ppermute(block, ("pp", "cp"), route)


def row_to_column(row):
    count = row.shape[1]
    down = lax.broadcasted_iota(jnp.int32, (count, count), 0)
    across = lax.broadcasted_iota(jnp.int32, (count, count), 1)
    return jnp.sum(jnp.where(down == across, row, 0), axis=1, keepdims=True)


def rank_in_row(row):
    count = row.shape[1]
    down = lax.broadcasted_iota(jnp.int32, (count, count), 0)
    across = lax.broadcasted_iota(jnp.int32, (count, count), 1)
    hits = jnp.logical_and(row_to_column(row) == row, down < across)
    return jnp.sum(hits.astype(jnp.int32), axis=0, keepdims=True)


def one_hot(rank, match, height):
    ids = lax.broadcasted_iota(jnp.int32, (height, rank.shape[1]), 0)
    return jnp.logical_and(ids == rank, match).astype(jnp.float32).astype(jnp.bfloat16)


def in_vmem(array):
    return pltpu.with_memory_space_constraint(array, pltpu.VMEM)


def specs(space, count):
    return [pl.BlockSpec(memory_space=space)] * count


def make_ready(keys, values, pair_order, limits, route_rows, where, *, cycle_size, split_size, packed_rows):
    row_count, width = keys.shape
    sections = route_rows.shape[0]
    half = row_count // 2
    block_len = half // 2
    head_rows = row_count + 16
    total = cycle_size * packed_rows

    def kernel(where_ref, order_ref, limit_ref, k_ref, v_ref, r_ref, first_ref, rest_ref, pack_ref, mask_ref):
        section, place = where_ref[0], where_ref[1]
        first_ref[0:row_count, 0:HD] = k_ref[:, 0:HD]
        first_ref[0:row_count, HD : 2 * HD] = v_ref[:, 0:HD]
        spare = jnp.zeros((16 - sections, row_count), jnp.float32)
        sent = jnp.concatenate([r_ref[...].astype(jnp.float32), spare], axis=0).astype(jnp.bfloat16)
        first_ref[row_count:head_rows, 0:HD] = sent
        first_ref[row_count:head_rows, HD : 2 * HD] = jnp.zeros((16, HD), jnp.bfloat16)
        rest_ref[:, 0 : width - HD] = k_ref[:, HD:width]
        rest_ref[:, width - HD :] = v_ref[:, HD:width]
        chips = r_ref[pl.ds(section, 1), :] // split_size
        rank = rank_in_row(chips)
        none = jnp.zeros((packed_rows, half), jnp.float32)
        for mask in range(cycle_size):
            ids = lax.broadcasted_iota(jnp.int32, (packed_rows, row_count), 0)
            pick = jnp.logical_and(ids == rank, chips == (place ^ mask)).astype(jnp.float32)
            first, second = pick[:, :half], pick[:, half:]
            rows = slice(mask * packed_rows, (mask + 1) * packed_rows)
            later = slice(total + mask * packed_rows, total + (mask + 1) * packed_rows)
            pack_ref[rows, :] = jnp.concatenate([first, none, second, none], axis=1).astype(jnp.bfloat16)
            pack_ref[later, :] = jnp.concatenate([none, first, none, second], axis=1).astype(jnp.bfloat16)
        own = order_ref[section, place]
        lane = lax.broadcasted_iota(jnp.int32, (half, 2 * half), 1) % half
        query_pos = jnp.where(lane < block_len, own, 2 * cycle_size - 2 - own) * block_len + lane
        down = lax.broadcasted_iota(jnp.int32, (half, 2 * half), 0)
        for mask in range(cycle_size):
            pair = order_ref[section, place ^ mask]
            key_pos = jnp.where(down < block_len, pair, 2 * cycle_size - 2 - pair) * block_len + down
            for seq in range(2):
                allowed = jnp.logical_and(key_pos <= query_pos, key_pos < limit_ref[seq, section])
                mask_ref[seq, mask * half : (mask + 1) * half, :] = allowed.astype(jnp.float32)

    return pl.pallas_call(
        kernel,
        out_shape=(
            pltpu.VMEM((head_rows, 2 * HD), jnp.bfloat16),
            pltpu.VMEM((row_count, 2 * (width - HD)), jnp.bfloat16),
            pltpu.VMEM((2 * total, 2 * row_count), jnp.bfloat16),
            pltpu.VMEM((2, cycle_size * half, row_count), jnp.float32),
        ),
        in_specs=specs(pltpu.SMEM, 3) + specs(pltpu.VMEM, 3),
        out_specs=tuple(specs(pltpu.VMEM, 4)),
        name="make_ready",
    )(where, pair_order, limits, keys, values, route_rows)


def count_rows(route_rows, heads, *, cycle_size, split_size):
    sections, row_count = route_rows.shape

    def kernel(r_ref, *refs):
        head_refs, most_ref = refs[: cycle_size - 1], refs[cycle_size - 1]
        tables = [r_ref[...].astype(jnp.float32)]
        tables += [ref[row_count : row_count + 16, 0:row_count].astype(jnp.float32)[0:sections] for ref in head_refs]
        table = jnp.concatenate(tables, axis=0)
        most = jnp.zeros((sections * cycle_size, 1), jnp.float32)
        for chip in range(cycle_size):
            low = chip * split_size
            hits = jnp.logical_and(table >= low, table < low + split_size).astype(jnp.float32)
            most = jnp.maximum(most, jnp.sum(hits, axis=1, keepdims=True))
        most_ref[0] = jnp.max(most).astype(jnp.int32)

    return pl.pallas_call(
        kernel,
        out_shape=jax.ShapeDtypeStruct((1,), jnp.int32),
        in_specs=specs(pltpu.VMEM, cycle_size),
        out_specs=specs(pltpu.SMEM, 1)[0],
        name="count_rows",
    )(route_rows, *[in_vmem(head) for head in heads])


def make_unpack(route_rows, heads, where, *, cycle_size, split_size, packed_rows, capacity):
    sections, row_count = route_rows.shape
    slot_rows = cycle_size * capacity

    def kernel(where_ref, r_ref, *refs):
        head_refs, slots_ref = refs[: cycle_size - 1], refs[cycle_size - 1]
        place, core = where_ref[1], where_ref[2]
        source = (where_ref[0] + sections - 1) % sections
        slots_ref[...] = jnp.zeros(slots_ref.shape, jnp.bfloat16)
        for mask in range(cycle_size):
            if mask == 0:
                targets = r_ref[pl.ds(source, 1), :]
            else:
                block = head_refs[mask - 1][row_count : row_count + 16, 0:row_count].astype(jnp.float32)
                ids = lax.broadcasted_iota(jnp.int32, block.shape, 0)
                targets = jnp.sum(jnp.where(ids == source, block, 0.0), axis=0, keepdims=True)
                targets = targets.astype(jnp.int32)
            chips = targets // split_size
            packed = one_hot(rank_in_row(chips), chips == place, packed_rows)
            slots = rank_in_row(targets)
            for step, which in enumerate((core, 1 - core)):
                slotted = one_hot(slots, targets == place * split_size + which, capacity)
                at = pl.ds(pl.multiple_of((place ^ mask) * capacity, capacity), capacity)
                slots_ref[step, at, mask * packed_rows : (mask + 1) * packed_rows] = lax.dot_general(
                    slotted, packed, (((1,), (1,)), ((), ())), preferred_element_type=jnp.float32
                ).astype(jnp.bfloat16)

    return pl.pallas_call(
        kernel,
        out_shape=pltpu.VMEM((split_size, slot_rows, cycle_size * packed_rows), jnp.bfloat16),
        in_specs=specs(pltpu.SMEM, 1) + specs(pltpu.VMEM, cycle_size),
        out_specs=specs(pltpu.VMEM, 1)[0],
        name="make_unpack",
    )(where, route_rows, *[in_vmem(head) for head in heads])


def attend(queries, pieces, pack, allow, group, *, cycle_size, group_size, packed_rows):
    row_count = queries.shape[0]
    half = row_count // 2
    total_rows = pack.shape[0] // 2
    stride = total_rows // cycle_size
    width = group_size * HD
    step_heads = min(8, group_size)
    step_width = step_heads * HD
    steps = group_size // step_heads
    scale = HD ** (-0.5)

    def kernel(q_hbm, pack_ref, allow_ref, *refs):
        kv_refs, out_refs = refs[:cycle_size], refs[cycle_size : 2 * cycle_size]
        q_ref, keys_ref, values_ref, sems = refs[2 * cycle_size :]
        for step in range(steps):
            at = group * width + step * step_width
            pltpu.make_async_copy(q_hbm.at[:, at : at + step_width], q_ref.at[step], sems.at[step]).start()

        seq_rows = [slice(seq * half, (seq + 1) * half) for seq in range(2)]
        for seq in range(2):
            for mask, (_, key_col, value_col) in enumerate(pieces):
                at = slice(mask * half, (mask + 1) * half)
                keys_ref[seq, at, :] = kv_refs[mask][seq_rows[seq], key_col : key_col + HD]
                values_ref[seq, :, at] = jnp.transpose(kv_refs[mask][seq_rows[seq], value_col : value_col + HD])

        def advance(step, carry):
            pltpu.make_async_copy(q_hbm.at[:, 0:step_width], q_ref.at[step], sems.at[step]).wait()
            attended = []
            for seq in range(2):
                q = jnp.concatenate(
                    [q_ref[step, seq_rows[seq], h * HD : (h + 1) * HD] for h in range(step_heads)], axis=0
                )
                scores = lax.dot_general(
                    keys_ref[seq], q, (((1,), (1,)), ((), ())), preferred_element_type=jnp.float32
                )
                tiles, totals = [], []
                for pair in range(step_heads // 2):
                    block = scores[:, pair * 2 * half : (pair + 1) * 2 * half] * scale
                    block = jnp.where(allow_ref[seq] > 0.0, block, masked_score)
                    block = jnp.exp(block - jnp.max(block, axis=0, keepdims=True))
                    totals.append(jnp.sum(block, axis=0, keepdims=True))
                    tiles.append(block.astype(jnp.bfloat16))
                weights = jnp.concatenate(tiles, axis=1)
                total = jnp.concatenate(totals, axis=1)
                summed = jnp.dot(values_ref[seq], weights, preferred_element_type=jnp.float32)
                attended.append((summed / total).astype(jnp.bfloat16))
            for pair in range(step_heads // 2):
                cols = slice(pair * 2 * half, (pair + 1) * 2 * half)
                both = jnp.concatenate([attended[0][:, cols], attended[1][:, cols]], axis=1)
                packed = lax.dot_general(
                    pack_ref[...], both, (((1,), (1,)), ((), ())), preferred_element_type=jnp.float32
                ).astype(jnp.bfloat16)
                for which in range(2):
                    head = pl.ds(pl.multiple_of(step * step_width + (2 * pair + which) * HD, HD), HD)
                    for mask in range(cycle_size):
                        at = which * total_rows + mask * stride
                        out_refs[mask][:, head] = packed[at : at + packed_rows]
            return carry

        lax.fori_loop(0, steps, advance, 0)

    return pl.pallas_call(
        kernel,
        in_specs=specs(pltpu.HBM, 1) + specs(pltpu.VMEM, 2 + cycle_size),
        out_specs=specs(pltpu.VMEM, cycle_size),
        out_shape=[pltpu.VMEM((packed_rows, width), jnp.bfloat16)] * cycle_size,
        scratch_shapes=[
            pltpu.VMEM((steps, row_count, step_width), jnp.bfloat16),
            pltpu.VMEM((2, cycle_size * half, HD), jnp.bfloat16),
            pltpu.VMEM((2, HD, cycle_size * half), jnp.bfloat16),
            pltpu.SemaphoreType.DMA((steps,)),
        ],
        compiler_params=pltpu.CompilerParams(vmem_limit_bytes=8 * 1024 * 1024),
        cost_estimate=pl.CostEstimate(flops=20000000000, transcendentals=0, bytes_accessed=0) if group == 0 else None,
        name="attend",
    )(queries, in_vmem(pack), in_vmem(allow), *[in_vmem(piece[0]) for piece in pieces])


def unpack_rows(received, slots, where, out, group, twins, *, group_count, own, twin):
    cycle_size = len(received)
    packed_rows, width = received[0].shape
    rows = slots.shape[1]
    spare = slots.shape[2] // cycle_size - packed_rows
    full = 2 * group_count * width
    tile = 512
    steps = width // tile

    def kernel(*refs):
        refs = list(refs)
        where_ref = refs.pop(0) if own else None
        in_refs = [refs.pop(0) for _ in range(cycle_size)]
        slots_ref = refs.pop(0)
        twin_refs = [refs.pop(0) for _ in twins]
        if own and out is not None:
            refs.pop(0)
        out_ref = refs.pop(0) if own else None
        send_ref = refs.pop(0) if twin else None
        own_ref, sems = refs if own else (None, None)

        def columns(which, index, step, size):
            at = (which * group_count + index) * width + step * size
            return pl.ds(pl.multiple_of(at, size), size)

        def copy(step):
            cols = pl.ds(pl.multiple_of(step * tile, tile), tile)
            at = columns(where_ref[2], group, step, tile)
            return pltpu.make_async_copy(own_ref.at[:, cols], out_ref.at[:, at], sems.at[step])

        def copy_twin(index):
            at = columns(1 - where_ref[2], index, 0, width)
            return pltpu.make_async_copy(twin_refs[index], out_ref.at[:, at], sems.at[steps + index])

        def advance(step, carry):
            cols = pl.ds(pl.multiple_of(step * tile, tile), tile)
            blocks = []
            for ref in in_refs:
                blocks.append(ref[:, cols])
                if spare:
                    blocks.append(jnp.zeros((spare, tile), jnp.bfloat16))
            block = jnp.concatenate(blocks, axis=0)
            if own:
                placed = jnp.dot(slots_ref[0], block, preferred_element_type=jnp.float32)
                own_ref[:, cols] = placed.astype(jnp.bfloat16)
                copy(step).start()
            if twin:
                placed = jnp.dot(slots_ref[1], block, preferred_element_type=jnp.float32)
                send_ref[:, cols] = placed.astype(jnp.bfloat16)
            return carry

        for index in range(len(twins)):
            copy_twin(index).start()
        lax.fori_loop(0, steps, advance, 0)
        if own:
            for step in range(steps):
                copy(step).wait()
        for index in range(len(twins)):
            copy_twin(index).wait()

    in_specs, args, aliases, out_specs, out_shape, scratch = [], [], {}, [], [], []
    if own:
        in_specs += specs(pltpu.SMEM, 1)
        args.append(where)
    in_specs += specs(pltpu.VMEM, cycle_size + 1 + len(twins))
    args += [in_vmem(block) for block in list(received) + [slots] + list(twins)]
    if own:
        if out is not None:
            in_specs += specs(pl.ANY, 1)
            aliases = {len(args): 0}
            args.append(out)
        out_specs += specs(pl.ANY, 1)
        out_shape.append(jax.ShapeDtypeStruct((rows, full), jnp.bfloat16))
        scratch = [
            pltpu.VMEM((rows, width), jnp.bfloat16),
            pltpu.SemaphoreType.DMA((steps + len(twins),)),
        ]
    if twin:
        out_specs += specs(pltpu.VMEM, 1)
        out_shape.append(pltpu.VMEM((rows, width), jnp.bfloat16))
    return pl.pallas_call(
        kernel,
        in_specs=in_specs,
        out_specs=out_specs,
        scratch_shapes=scratch,
        out_shape=out_shape,
        input_output_aliases=aliases,
        compiler_params=pltpu.CompilerParams(vmem_limit_bytes=8 * 1024 * 1024),
        name="unpack_rows",
    )(*args)


def place_twin(block, out, where, group, *, group_count):
    width = block.shape[1]

    def kernel(where_ref, in_ref, old_ref, out_ref, sem):
        at = pl.multiple_of(((1 - where_ref[2]) * group_count + group) * width, width)
        copy = pltpu.make_async_copy(in_ref, out_ref.at[:, pl.ds(at, width)], sem)
        copy.start()
        copy.wait()

    return pl.pallas_call(
        kernel,
        in_specs=specs(pltpu.SMEM, 1) + specs(pltpu.VMEM, 1) + specs(pl.ANY, 1),
        out_specs=specs(pl.ANY, 1)[0],
        scratch_shapes=[pltpu.SemaphoreType.DMA(())],
        out_shape=jax.ShapeDtypeStruct(out.shape, out.dtype),
        input_output_aliases={2: 0},
        compiler_params=pltpu.CompilerParams(vmem_limit_bytes=8 * 1024 * 1024),
        name="place_twin",
    )(where, in_vmem(block), out)


def body(queries, keys, values, pair_order, lengths, routes):
    cycle_size = lax.axis_size("cp")
    split_size = lax.axis_size("tp")
    row_count, width = queries.shape
    group_count = keys.shape[1] // HD
    group_size = width // keys.shape[1]
    dest_count = cycle_size * split_size
    capacity = 2 * row_count // dest_count
    most_rows = min(row_count, split_size * capacity)
    masks = [2, 3, 1, 0]
    where = jnp.stack([lax.axis_index("pp"), lax.axis_index("cp"), lax.axis_index("tp")]).astype(jnp.int32)
    route_rows = routes[:, :, 0]
    sizes = dict(cycle_size=cycle_size, split_size=split_size, packed_rows=most_rows)
    heads_of = dict(cycle_size=cycle_size, group_size=group_size)
    head, rest, pack, allow = make_ready(keys, values, pair_order, lengths.T, route_rows, where, **sizes)
    heads = [head] + [to_partner(head, mask) for mask in range(1, cycle_size)]
    rests = [rest] + [to_partner(rest, mask) for mask in (1, 2)]
    most = count_rows(route_rows, heads[1:], cycle_size=cycle_size, split_size=split_size)
    pieces = [(piece, 0, HD) for piece in heads]
    leading = attend(queries, pieces, pack, allow, 0, packed_rows=most_rows, **heads_of)

    def deliver(packed_rows, queries, pack, allow, route_rows, where, heads, rests, leading):
        rests = rests + [to_partner(rests[2], 1)]
        arrived = []
        for group in range(group_count):
            if group == 0:
                packed = [block[:packed_rows] for block in leading]
            else:
                first = (group - 1) * HD
                pieces = [(piece, first, first + keys.shape[1] - HD) for piece in rests]
                packed = attend(queries, pieces, pack, allow, group, packed_rows=packed_rows, **heads_of)
            sent = {mask: to_next_section(packed[mask], mask) for mask in masks}
            arrived.append([sent[mask] for mask in range(cycle_size)])
        slots = make_unpack(route_rows, heads, where, capacity=capacity, **sizes)
        out, twins = None, []
        swap = [(0, 1), (1, 0)]
        for group in range(group_count - 1):
            out, send = unpack_rows(
                arrived[group], slots, where, out, group, [], group_count=group_count, own=True, twin=True
            )
            twins.append(lax.ppermute(send, "tp", swap))
        last = group_count - 1
        (send,) = unpack_rows(
            arrived[last], slots, where, None, last, [], group_count=group_count, own=False, twin=True
        )
        late = lax.ppermute(send, "tp", swap)
        (out,) = unpack_rows(
            arrived[last], slots, where, out, last, twins, group_count=group_count, own=True, twin=False
        )
        return place_twin(late, out, where, last, group_count=group_count)

    heights = [most_rows * 3 // 4, most_rows * 7 // 8, most_rows]
    choice = sum((most[0] > height).astype(jnp.int32) for height in heights[:-1])
    branches = [lambda *args, height=height: deliver(height, *args) for height in heights]
    return lax.switch(choice, branches, queries, pack, allow, route_rows, where, heads[1:], rests, leading)


def solution(mesh):
    placed = (
        P(("pp", "cp"), "tp"),
        P(("pp", "cp"), "tp"),
        P(("pp", "cp"), "tp"),
        P(),
        P(),
        P(None, "cp", None),
    )
    small = mesh.shape["cp"] == 4 and mesh.shape["tp"] == 2
    return jax.shard_map(
        body if small else general_body,
        mesh=mesh,
        in_specs=placed,
        out_specs=P(("pp", "cp", "tp"), None),
        check_vma=False,
    )
```

profile of v0, /device:TPU:7, one launch (start us, length us, event | category | flops | bytes accessed | tf_op | source)
XLA Modules:
  0.0 104.7 jit_solution(1680402425331142759)
XLA Ops:
  1.3 1.4 %collective-permute-start.63 = (bf16[144,256]{1,0:T(8,128)(2,1)S(1)}, bf16[144,256]{1,0:T(8,128)(2,1)S(1)}, u32[]{:S(2)}, u32[]{:S(2)}) collective-permute-start(bf16[144,256]{1,0:T(8,128)(2,1)S(1)} %get-tuple-element.206.refs_0_), channel_id=1, source_target_pairs={{0,2},{2,0},{4,6},{6,4},{1,3},{3,1},{5,7},{7,5},{8,10},{10,8},{12,... | collective-permute-start | bytes 221192 | tf_op jit(solution)/shard_map/ppermute | solution.py:125
  2.7 2.3 %collective-permute-start.64 = (bf16[144,256]{1,0:T(8,128)(2,1)S(1)}, bf16[144,256]{1,0:T(8,128)(2,1)S(1)}, u32[]{:S(2)}, u32[]{:S(2)}) collective-permute-start(bf16[144,256]{1,0:T(8,128)(2,1)S(1)} %get-tuple-element.206.refs_0_), channel_id=1, source_target_pairs={{0,4},{2,6},{4,0},{6,2},{1,5},{3,7},{5,1},{7,3},{8,12},{10,14},{12... | collective-permute-start | bytes 221192 | tf_op jit(solution)/shard_map/ppermute | solution.py:125
  6.3 2.2 %collective-permute-start.67 = (bf16[128,768]{1,0:T(8,128)(2,1)S(1)}, bf16[128,768]{1,0:T(8,128)(2,1)S(1)}, u32[]{:S(2)}, u32[]{:S(2)}) collective-permute-start(bf16[128,768]{1,0:T(8,128)(2,1)S(1)} %get-tuple-element.207), channel_id=1, source_target_pairs={{0,2},{2,0},{4,6},{6,4},{1,3},{3,1},{5,7},{7,5},{8,10},{10,8},{12,... | collective-permute-start | bytes 589832 | tf_op jit(solution)/shard_map/ppermute | solution.py:125
  8.5 1.5 %collective-permute-done.65.refs_2_.refs_3_ = bf16[144,256]{1,0:T(8,128)(2,1)S(1)} collective-permute-done((bf16[144,256]{1,0:T(8,128)(2,1)S(1)}, bf16[144,256]{1,0:T(8,128)(2,1)S(1)}, u32[]{:S(2)}, u32[]{:S(2)}) %collective-permute-start.65) | collective-permute-done | bytes 73760 | tf_op jit(solution)/shard_map/ppermute | solution.py:125
  10.0 3.5 %attend.19 = (bf16[64,2048]{1,0:T(8,128)(2,1)S(1)}, bf16[64,2048]{1,0:T(8,128)(2,1)S(1)}, bf16[64,2048]{1,0:T(8,128)(2,1)S(1)}, bf16[64,2048]{1,0:T(8,128)(2,1)S(1)}) custom-call(bf16[128,8192]{1,0:T(8,128)(2,1)} %q_hbm.1, bf16[512,256]{1,0:T(8,128)(2,1)S(1)} %get-tuple-element.208.pack_ref, f32[2,256,128]{2,1,0:T(8,128)S(1)} %get-tuple-element.209.allow_ref, ...), custom_call_target="tpu_custom_call" | custom-call | flops 20000000000 | tf_op jit(solution)/shard_map/attend/pallas_call | solution.py:341
  16.1 4.0 %collective-permute-done.66 = bf16[128,768]{1,0:T(8,128)(2,1)S(1)} collective-permute-done((bf16[128,768]{1,0:T(8,128)(2,1)S(1)}, bf16[128,768]{1,0:T(8,128)(2,1)S(1)}, u32[]{:S(2)}, u32[]{:S(2)}) %collective-permute-start.66) | collective-permute-done | bytes 196640 | tf_op jit(solution)/shard_map/ppermute | solution.py:125
  20.1 84.4 %conditional.1 = (bf16[128,16384]{1,0:T(8,128)(2,1)}) conditional(s32[]{:T(128)} %bitcast.5, (bf16[128,768]{1,0:T(8,128)(2,1)S(1)}, bf16[128,8192]{1,0:T(8,128)(2,1)}, bf16[512,256]{1,0:T(8,128)(2,1)S(1)}, f32[2,256,128]{2,1,0:T(8,128)S(1)}, bf16[128,768]{1,0:T(8,128)(2,1)S(1)}, /*index=5*/bf16[128,768]{1,0:T(8,128)(2,1)S(1)}, ...), branch_computations={%region_0.0_spmd, %region_1.0_spmd, %region_2.0_spmd} | conditional | bytes 42738944 | solution.py:525
  22.9 3.5 %collective-permute-start.8 = (bf16[48,2048]{1,0:T(8,128)(2,1)S(1)}, bf16[48,2048]{1,0:T(8,128)(2,1)S(1)}, u32[]{:S(2)}, u32[]{:S(2)}) collective-permute-start(bf16[48,2048]{1,0:T(8,128)(2,1)S(1)} %slice.18), channel_id=1, source_target_pairs={{0,12},{2,14},{4,8},{6,10},{8,20},{10,22},{12,16},{14,18},{16,28},... | collective-permute-start | bytes 589832 | tf_op jit(solution)/shard_map/cond/branch_0_fun/ppermute | solution.py:135
  26.4 1.7 %collective-permute-start.9 = (bf16[48,2048]{1,0:T(8,128)(2,1)S(1)}, bf16[48,2048]{1,0:T(8,128)(2,1)S(1)}, u32[]{:S(2)}, u32[]{:S(2)}) collective-permute-start(bf16[48,2048]{1,0:T(8,128)(2,1)S(1)} %slice.19), channel_id=1, source_target_pairs={{0,14},{2,12},{4,10},{6,8},{8,22},{10,20},{12,18},{14,16},{16,30},... | collective-permute-start | bytes 589832 | tf_op jit(solution)/shard_map/cond/branch_0_fun/ppermute | solution.py:135
  28.1 3.6 %attend.11 = (bf16[48,2048]{1,0:T(8,128)(2,1)S(1)}, bf16[48,2048]{1,0:T(8,128)(2,1)S(1)}, bf16[48,2048]{1,0:T(8,128)(2,1)S(1)}, bf16[48,2048]{1,0:T(8,128)(2,1)S(1)}) custom-call(bf16[128,8192]{1,0:T(8,128)(2,1)} %get-tuple-element.100.q_hbm, bf16[512,256]{1,0:T(8,128)(2,1)S(1)} %get-tuple-element.101.pack_ref, ...), custom_call_target="tpu_custom_call" | custom-call | tf_op jit(solution)/shard_map/cond/branch_0_fun/attend/pallas_call | solution.py:341
  32.3 3.5 %attend.12 = (bf16[48,2048]{1,0:T(8,128)(2,1)S(1)}, bf16[48,2048]{1,0:T(8,128)(2,1)S(1)}, bf16[48,2048]{1,0:T(8,128)(2,1)S(1)}, bf16[48,2048]{1,0:T(8,128)(2,1)}) custom-call(bf16[128,8192]{1,0:T(8,128)(2,1)S(1)} %copy-done.16, bf16[512,256]{1,0:T(8,128)(2,1)S(1)} %get-tuple-element.101.pack_ref, f32[2,256,128]{2,1,0:T(8,128)S(1)} %get-tuple-element.102.allow_ref, ...), custom_call_target="tpu_custom_call" | custom-call | tf_op jit(solution)/shard_map/cond/branch_0_fun/attend/pallas_call | solution.py:341
  35.9 4.4 %collective-permute-start.13 = (bf16[48,2048]{1,0:T(8,128)(2,1)S(1)}, bf16[48,2048]{1,0:T(8,128)(2,1)S(1)}, u32[]{:S(2)}, u32[]{:S(2)}) collective-permute-start(bf16[48,2048]{1,0:T(8,128)(2,1)S(1)} %get-tuple-element.121), channel_id=1, source_target_pairs={{0,12},{2,14},{4,8},{6,10},{8,20},{10,22},{12,16},{14,18},{16,28},... | collective-permute-start | bytes 589832 | tf_op jit(solution)/shard_map/cond/branch_0_fun/ppermute | solution.py:135
  40.2 1.6 %collective-permute-start.14 = (bf16[48,2048]{1,0:T(8,128)(2,1)S(1)}, bf16[48,2048]{1,0:T(8,128)(2,1)S(1)}, u32[]{:S(2)}, u32[]{:S(2)}) collective-permute-start(bf16[48,2048]{1,0:T(8,128)(2,1)S(1)} %get-tuple-element.122), channel_id=1, source_target_pairs={{0,14},{2,12},{4,10},{6,8},{8,22},{10,20},{12,18},{14,16},{16,30},... | collective-permute-start | bytes 589832 | tf_op jit(solution)/shard_map/cond/branch_0_fun/ppermute | solution.py:135
  42.1 10.7 %collective-permute-done.11.refs_1_ = bf16[48,2048]{1,0:T(8,128)(2,1)S(1)} collective-permute-done((bf16[48,2048]{1,0:T(8,128)(2,1)S(1)}, bf16[48,2048]{1,0:T(8,128)(2,1)S(1)}, u32[]{:S(2)}, u32[]{:S(2)}) %collective-permute-start.11) | collective-permute-done | bytes 196640 | tf_op jit(solution)/shard_map/cond/branch_0_fun/ppermute | solution.py:135
  52.8 4.3 %collective-permute-start.18 = (bf16[48,2048]{1,0:T(8,128)(2,1)S(1)}, bf16[48,2048]{1,0:T(8,128)(2,1)S(1)}, u32[]{:S(2)}, u32[]{:S(2)}) collective-permute-start(bf16[48,2048]{1,0:T(8,128)(2,1)S(1)} %get-tuple-element.127), channel_id=1, source_target_pairs={{0,12},{2,14},{4,8},{6,10},{8,20},{10,22},{12,16},{14,18},{16,28},... | collective-permute-start | bytes 589832 | tf_op jit(solution)/shard_map/cond/branch_0_fun/ppermute | solution.py:135
  57.1 3.7 %attend.10 = (bf16[48,2048]{1,0:T(8,128)(2,1)}, bf16[48,2048]{1,0:T(8,128)(2,1)}, bf16[48,2048]{1,0:T(8,128)(2,1)}, bf16[48,2048]{1,0:T(8,128)(2,1)}) custom-call(bf16[128,8192]{1,0:T(8,128)(2,1)S(1)} %copy-done.16, bf16[512,256]{1,0:T(8,128)(2,1)S(1)} %get-tuple-element.101.pack_ref, f32[2,256,128]{2,1,0:T(8,128)S(1)} %get-tuple-element.102.allow_ref, ...), custom_call_target="tpu_custom_call" | custom-call | tf_op jit(solution)/shard_map/cond/branch_0_fun/attend/pallas_call | solution.py:341
  60.8 2.7 %collective-permute-start.19 = (bf16[48,2048]{1,0:T(8,128)(2,1)}, bf16[48,2048]{1,0:T(8,128)(2,1)}, u32[]{:S(2)}, u32[]{:S(2)}) collective-permute-start(bf16[48,2048]{1,0:T(8,128)(2,1)} %get-tuple-element.128), channel_id=1, source_target_pairs={{0,14},{2,12},{4,10},{6,8},{8,22},{10,20},{12,18},{14,16},{16,30},... | collective-permute-start | bytes 589832 | tf_op jit(solution)/shard_map/cond/branch_0_fun/ppermute | solution.py:135
  64.5 3.0 %collective-permute-start.3 = (bf16[48,2048]{1,0:T(8,128)(2,1)}, bf16[48,2048]{1,0:T(8,128)(2,1)S(1)}, u32[]{:S(2)}, u32[]{:S(2)}) collective-permute-start(bf16[48,2048]{1,0:T(8,128)(2,1)} %get-tuple-element.108), channel_id=1, source_target_pairs={{0,12},{2,14},{4,8},{6,10},{8,20},{10,22},{12,16},{14,18},{16,28},... | collective-permute-start | bytes 589832 | tf_op jit(solution)/shard_map/cond/branch_0_fun/ppermute | solution.py:135
  68.2 10.8 %collective-permute-start.4 = (bf16[48,2048]{1,0:T(8,128)(2,1)}, bf16[48,2048]{1,0:T(8,128)(2,1)S(1)}, u32[]{:S(2)}, u32[]{:S(2)}) collective-permute-start(bf16[48,2048]{1,0:T(8,128)(2,1)} %get-tuple-element.109), channel_id=1, source_target_pairs={{0,14},{2,12},{4,10},{6,8},{8,22},{10,20},{12,18},{14,16},{16,30},... | collective-permute-start | bytes 589832 | tf_op jit(solution)/shard_map/cond/branch_0_fun/ppermute | solution.py:135
  80.2 2.2 %unpack_rows.16 = (bf16[128,16384]{1,0:T(8,128)(2,1)}, bf16[128,2048]{1,0:T(8,128)(2,1)S(1)}) custom-call(s32[3]{0:T(128)} %copy-done.19, bf16[48,2048]{1,0:T(8,128)(2,1)S(1)} %collective-permute-done.6.refs_1_, bf16[48,2048]{1,0:T(8,128)(2,1)S(1)} %collective-permute-done.7.refs_2_, bf16[48,2048]{1,0:T(8,128)(2,1)S(1)} %collective-permute-done.8.refs_3_, ...), custom_call_target="tpu_custom_call" | custom-call | tf_op jit(solution)/shard_map/cond/branch_0_fun/unpack_rows/pallas_call | solution.py:438
  82.5 2.2 %unpack_rows.17 = (bf16[128,16384]{1,0:T(8,128)(2,1)}, bf16[128,2048]{1,0:T(8,128)(2,1)S(1)}) custom-call(s32[3]{0:T(128)} %copy-done.19, bf16[48,2048]{1,0:T(8,128)(2,1)S(1)} %collective-permute-done.11.refs_1_, bf16[48,2048]{1,0:T(8,128)(2,1)S(1)} %collective-permute-done.12.refs_2_, ...), custom_call_target="tpu_custom_call", output_to_operand_aliasing={{0}: (6, {})} | custom-call | tf_op jit(solution)/shard_map/cond/branch_0_fun/unpack_rows/pallas_call | solution.py:438
  84.7 10.8 %collective-permute-start.10 = (bf16[128,2048]{1,0:T(8,128)(2,1)S(1)}, bf16[128,2048]{1,0:T(8,128)(2,1)S(1)}, u32[]{:S(2)}, u32[]{:S(2)}) collective-permute-start(bf16[128,2048]{1,0:T(8,128)(2,1)S(1)} %get-tuple-element.118), channel_id=1, source_target_pairs={{0,1},{1,0},{2,3},{3,2},{4,5},{5,4},{6,7},{7,6},{8,9},{9,8},{10,11... | collective-permute-start | bytes 1572872 | tf_op jit(solution)/shard_map/cond/branch_0_fun/ppermute | solution.py:511
  95.6 2.5 %unpack_rows.18 = (bf16[128,16384]{1,0:T(8,128)(2,1)}, bf16[128,2048]{1,0:T(8,128)(2,1)S(1)}) custom-call(s32[3]{0:T(128)} %copy-done.19, bf16[48,2048]{1,0:T(8,128)(2,1)S(1)} %collective-permute-done.16.refs_1_, bf16[48,2048]{1,0:T(8,128)(2,1)S(1)} %collective-permute-done.17.refs_2_, ...), custom_call_target="tpu_custom_call", output_to_operand_aliasing={{0}: (6, {})} | custom-call | tf_op jit(solution)/shard_map/cond/branch_0_fun/unpack_rows/pallas_call | solution.py:438
  100.8 2.0 %unpack_rows.19.old_ref = bf16[128,16384]{1,0:T(8,128)(2,1)} custom-call(s32[3]{0:T(128)S(1)} %copy-done.20, bf16[48,2048]{1,0:T(8,128)(2,1)S(1)} %collective-permute-done.1.refs_0_.refs_1_, bf16[48,2048]{1,0:T(8,128)(2,1)S(1)} %collective-permute-done.2.refs_1_.refs_2_, ...), custom_call_target="tpu_custom_call", output_to_operand_aliasing={{}: (9, {})} | custom-call | tf_op jit(solution)/shard_map/cond/branch_0_fun/unpack_rows/pallas_call | solution.py:438
  (57 shorter events, 14.7 us)
Async XLA Ops:
  1.3 7.2 %collective-permute-start.63 = (bf16[144,256]{1,0:T(8,128)(2,1)S(1)}, bf16[144,256]{1,0:T(8,128)(2,1)S(1)}, u32[]{:S(2)}, u32[]{:S(2)}) collective-permute-start(bf16[144,256]{1,0:T(8,128)(2,1)S(1)} %get-tuple-element.206.refs_0_), channel_id=1, source_target_pairs={{0,2},{2,0},{4,6},{6,4},{1,3},{3,1},{5,7},{7,5},{8,10},{10,8},{12,... | collective-permute-start | bytes 221192 | tf_op jit(solution)/shard_map/ppermute | solution.py:125
  2.7 5.9 %collective-permute-start.64 = (bf16[144,256]{1,0:T(8,128)(2,1)S(1)}, bf16[144,256]{1,0:T(8,128)(2,1)S(1)}, u32[]{:S(2)}, u32[]{:S(2)}) collective-permute-start(bf16[144,256]{1,0:T(8,128)(2,1)S(1)} %get-tuple-element.206.refs_0_), channel_id=1, source_target_pairs={{0,4},{2,6},{4,0},{6,2},{1,5},{3,7},{5,1},{7,3},{8,12},{10,14},{12... | collective-permute-start | bytes 221192 | tf_op jit(solution)/shard_map/ppermute | solution.py:125
  5.0 5.1 %collective-permute-start.65 = (bf16[144,256]{1,0:T(8,128)(2,1)S(1)}, bf16[144,256]{1,0:T(8,128)(2,1)S(1)}, u32[]{:S(2)}, u32[]{:S(2)}) collective-permute-start(bf16[144,256]{1,0:T(8,128)(2,1)S(1)} %get-tuple-element.206.refs_0_), channel_id=1, source_target_pairs={{0,6},{2,4},{4,2},{6,0},{1,7},{3,5},{5,3},{7,1},{8,14},{10,12},{12... | collective-permute-start | bytes 221192 | tf_op jit(solution)/shard_map/ppermute | solution.py:125
  5.0 15.1 %collective-permute-start.66 = (bf16[128,768]{1,0:T(8,128)(2,1)S(1)}, bf16[128,768]{1,0:T(8,128)(2,1)S(1)}, u32[]{:S(2)}, u32[]{:S(2)}) collective-permute-start(bf16[128,768]{1,0:T(8,128)(2,1)S(1)} %get-tuple-element.207), channel_id=1, source_target_pairs={{0,4},{2,6},{4,0},{6,2},{1,5},{3,7},{5,1},{7,3},{8,12},{10,14},{12... | collective-permute-start | bytes 589832 | tf_op jit(solution)/shard_map/ppermute | solution.py:125
  6.3 13.8 %collective-permute-start.67 = (bf16[128,768]{1,0:T(8,128)(2,1)S(1)}, bf16[128,768]{1,0:T(8,128)(2,1)S(1)}, u32[]{:S(2)}, u32[]{:S(2)}) collective-permute-start(bf16[128,768]{1,0:T(8,128)(2,1)S(1)} %get-tuple-element.207), channel_id=1, source_target_pairs={{0,2},{2,0},{4,6},{6,4},{1,3},{3,1},{5,7},{7,5},{8,10},{10,8},{12,... | collective-permute-start | bytes 589832 | tf_op jit(solution)/shard_map/ppermute | solution.py:125
  20.1 8.0 %collective-permute-start = (bf16[128,768]{1,0:T(8,128)(2,1)S(1)}, bf16[128,768]{1,0:T(8,128)(2,1)S(1)}, u32[]{:S(2)}, u32[]{:S(2)}) collective-permute-start(bf16[128,768]{1,0:T(8,128)(2,1)S(1)} %get-tuple-element.105.refs_2_), channel_id=1, source_target_pairs={{0,2},{2,0},{4,6},{6,4},{1,3},{3,1},{5,7},{7,5},{8,10},{10,8},{12,... | collective-permute-start | bytes 589832 | tf_op jit(solution)/shard_map/cond/branch_0_fun/ppermute | solution.py:125
  21.3 10.6 %collective-permute-start.6 = (bf16[48,2048]{1,0:T(8,128)(2,1)S(1)}, bf16[48,2048]{1,0:T(8,128)(2,1)S(1)}, u32[]{:S(2)}, u32[]{:S(2)}) collective-permute-start(bf16[48,2048]{1,0:T(8,128)(2,1)S(1)} %slice.16), channel_id=1, source_target_pairs={{0,8},{2,10},{4,12},{6,14},{8,16},{10,18},{12,20},{14,22},{16,24},... | collective-permute-start | bytes 589832 | tf_op jit(solution)/shard_map/cond/branch_0_fun/ppermute | solution.py:135
  21.6 14.3 %collective-permute-start.7 = (bf16[48,2048]{1,0:T(8,128)(2,1)S(1)}, bf16[48,2048]{1,0:T(8,128)(2,1)S(1)}, u32[]{:S(2)}, u32[]{:S(2)}) collective-permute-start(bf16[48,2048]{1,0:T(8,128)(2,1)S(1)} %slice.17), channel_id=1, source_target_pairs={{0,10},{2,8},{4,14},{6,12},{8,18},{10,16},{12,22},{14,20},{16,26},... | collective-permute-start | bytes 589832 | tf_op jit(solution)/shard_map/cond/branch_0_fun/ppermute | solution.py:135
  22.9 17.3 %collective-permute-start.8 = (bf16[48,2048]{1,0:T(8,128)(2,1)S(1)}, bf16[48,2048]{1,0:T(8,128)(2,1)S(1)}, u32[]{:S(2)}, u32[]{:S(2)}) collective-permute-start(bf16[48,2048]{1,0:T(8,128)(2,1)S(1)} %slice.18), channel_id=1, source_target_pairs={{0,12},{2,14},{4,8},{6,10},{8,20},{10,22},{12,16},{14,18},{16,28},... | collective-permute-start | bytes 589832 | tf_op jit(solution)/shard_map/cond/branch_0_fun/ppermute | solution.py:135
  26.4 15.5 %collective-permute-start.9 = (bf16[48,2048]{1,0:T(8,128)(2,1)S(1)}, bf16[48,2048]{1,0:T(8,128)(2,1)S(1)}, u32[]{:S(2)}, u32[]{:S(2)}) collective-permute-start(bf16[48,2048]{1,0:T(8,128)(2,1)S(1)} %slice.19), channel_id=1, source_target_pairs={{0,14},{2,12},{4,10},{6,8},{8,22},{10,20},{12,18},{14,16},{16,30},... | collective-permute-start | bytes 589832 | tf_op jit(solution)/shard_map/cond/branch_0_fun/ppermute | solution.py:135
  31.7 21.1 %collective-permute-start.11 = (bf16[48,2048]{1,0:T(8,128)(2,1)S(1)}, bf16[48,2048]{1,0:T(8,128)(2,1)S(1)}, u32[]{:S(2)}, u32[]{:S(2)}) collective-permute-start(bf16[48,2048]{1,0:T(8,128)(2,1)S(1)} %get-tuple-element.119), channel_id=1, source_target_pairs={{0,8},{2,10},{4,12},{6,14},{8,16},{10,18},{12,20},{14,22},{16,24},... | collective-permute-start | bytes 589832 | tf_op jit(solution)/shard_map/cond/branch_0_fun/ppermute | solution.py:135
  32.0 20.8 %collective-permute-start.12 = (bf16[48,2048]{1,0:T(8,128)(2,1)S(1)}, bf16[48,2048]{1,0:T(8,128)(2,1)S(1)}, u32[]{:S(2)}, u32[]{:S(2)}) collective-permute-start(bf16[48,2048]{1,0:T(8,128)(2,1)S(1)} %get-tuple-element.120), channel_id=1, source_target_pairs={{0,10},{2,8},{4,14},{6,12},{8,18},{10,16},{12,22},{14,20},{16,26},... | collective-permute-start | bytes 589832 | tf_op jit(solution)/shard_map/cond/branch_0_fun/ppermute | solution.py:135
  35.9 24.9 %collective-permute-start.13 = (bf16[48,2048]{1,0:T(8,128)(2,1)S(1)}, bf16[48,2048]{1,0:T(8,128)(2,1)S(1)}, u32[]{:S(2)}, u32[]{:S(2)}) collective-permute-start(bf16[48,2048]{1,0:T(8,128)(2,1)S(1)} %get-tuple-element.121), channel_id=1, source_target_pairs={{0,12},{2,14},{4,8},{6,10},{8,20},{10,22},{12,16},{14,18},{16,28},... | collective-permute-start | bytes 589832 | tf_op jit(solution)/shard_map/cond/branch_0_fun/ppermute | solution.py:135
  40.2 23.2 %collective-permute-start.14 = (bf16[48,2048]{1,0:T(8,128)(2,1)S(1)}, bf16[48,2048]{1,0:T(8,128)(2,1)S(1)}, u32[]{:S(2)}, u32[]{:S(2)}) collective-permute-start(bf16[48,2048]{1,0:T(8,128)(2,1)S(1)} %get-tuple-element.122), channel_id=1, source_target_pairs={{0,14},{2,12},{4,10},{6,8},{8,22},{10,20},{12,18},{14,16},{16,30},... | collective-permute-start | bytes 589832 | tf_op jit(solution)/shard_map/cond/branch_0_fun/ppermute | solution.py:135
  41.9 21.6 %collective-permute-start.16 = (bf16[48,2048]{1,0:T(8,128)(2,1)S(1)}, bf16[48,2048]{1,0:T(8,128)(2,1)S(1)}, u32[]{:S(2)}, u32[]{:S(2)}) collective-permute-start(bf16[48,2048]{1,0:T(8,128)(2,1)S(1)} %get-tuple-element.125), channel_id=1, source_target_pairs={{0,8},{2,10},{4,12},{6,14},{8,16},{10,18},{12,20},{14,22},{16,24},... | collective-permute-start | bytes 589832 | tf_op jit(solution)/shard_map/cond/branch_0_fun/ppermute | solution.py:135
  52.8 11.7 %collective-permute-start.17 = (bf16[48,2048]{1,0:T(8,128)(2,1)S(1)}, bf16[48,2048]{1,0:T(8,128)(2,1)S(1)}, u32[]{:S(2)}, u32[]{:S(2)}) collective-permute-start(bf16[48,2048]{1,0:T(8,128)(2,1)S(1)} %get-tuple-element.126), channel_id=1, source_target_pairs={{0,10},{2,8},{4,14},{6,12},{8,18},{10,16},{12,22},{14,20},{16,26},... | collective-permute-start | bytes 589832 | tf_op jit(solution)/shard_map/cond/branch_0_fun/ppermute | solution.py:135
  52.8 14.7 %collective-permute-start.18 = (bf16[48,2048]{1,0:T(8,128)(2,1)S(1)}, bf16[48,2048]{1,0:T(8,128)(2,1)S(1)}, u32[]{:S(2)}, u32[]{:S(2)}) collective-permute-start(bf16[48,2048]{1,0:T(8,128)(2,1)S(1)} %get-tuple-element.127), channel_id=1, source_target_pairs={{0,12},{2,14},{4,8},{6,10},{8,20},{10,22},{12,16},{14,18},{16,28},... | collective-permute-start | bytes 589832 | tf_op jit(solution)/shard_map/cond/branch_0_fun/ppermute | solution.py:135
  60.8 24.0 %collective-permute-start.19 = (bf16[48,2048]{1,0:T(8,128)(2,1)}, bf16[48,2048]{1,0:T(8,128)(2,1)}, u32[]{:S(2)}, u32[]{:S(2)}) collective-permute-start(bf16[48,2048]{1,0:T(8,128)(2,1)} %get-tuple-element.128), channel_id=1, source_target_pairs={{0,14},{2,12},{4,10},{6,8},{8,22},{10,20},{12,18},{14,16},{16,30},... | collective-permute-start | bytes 589832 | tf_op jit(solution)/shard_map/cond/branch_0_fun/ppermute | solution.py:135
  63.4 34.6 %collective-permute-start.1 = (bf16[48,2048]{1,0:T(8,128)(2,1)}, bf16[48,2048]{1,0:T(8,128)(2,1)S(1)}, u32[]{:S(2)}, u32[]{:S(2)}) collective-permute-start(bf16[48,2048]{1,0:T(8,128)(2,1)} %get-tuple-element.106), channel_id=1, source_target_pairs={{0,8},{2,10},{4,12},{6,14},{8,16},{10,18},{12,20},{14,22},{16,24},... | collective-permute-start | bytes 589832 | tf_op jit(solution)/shard_map/cond/branch_0_fun/ppermute | solution.py:135
  63.4 34.7 %collective-permute-start.2 = (bf16[48,2048]{1,0:T(8,128)(2,1)}, bf16[48,2048]{1,0:T(8,128)(2,1)S(1)}, u32[]{:S(2)}, u32[]{:S(2)}) collective-permute-start(bf16[48,2048]{1,0:T(8,128)(2,1)} %get-tuple-element.107), channel_id=1, source_target_pairs={{0,10},{2,8},{4,14},{6,12},{8,18},{10,16},{12,22},{14,20},{16,26},... | collective-permute-start | bytes 589832 | tf_op jit(solution)/shard_map/cond/branch_0_fun/ppermute | solution.py:135
  64.5 34.2 %collective-permute-start.3 = (bf16[48,2048]{1,0:T(8,128)(2,1)}, bf16[48,2048]{1,0:T(8,128)(2,1)S(1)}, u32[]{:S(2)}, u32[]{:S(2)}) collective-permute-start(bf16[48,2048]{1,0:T(8,128)(2,1)} %get-tuple-element.108), channel_id=1, source_target_pairs={{0,12},{2,14},{4,8},{6,10},{8,20},{10,22},{12,16},{14,18},{16,28},... | collective-permute-start | bytes 589832 | tf_op jit(solution)/shard_map/cond/branch_0_fun/ppermute | solution.py:135
  68.2 30.5 %collective-permute-start.4 = (bf16[48,2048]{1,0:T(8,128)(2,1)}, bf16[48,2048]{1,0:T(8,128)(2,1)S(1)}, u32[]{:S(2)}, u32[]{:S(2)}) collective-permute-start(bf16[48,2048]{1,0:T(8,128)(2,1)} %get-tuple-element.109), channel_id=1, source_target_pairs={{0,14},{2,12},{4,10},{6,8},{8,22},{10,20},{12,18},{14,16},{16,30},... | collective-permute-start | bytes 589832 | tf_op jit(solution)/shard_map/cond/branch_0_fun/ppermute | solution.py:135
  84.7 14.9 %collective-permute-start.10 = (bf16[128,2048]{1,0:T(8,128)(2,1)S(1)}, bf16[128,2048]{1,0:T(8,128)(2,1)S(1)}, u32[]{:S(2)}, u32[]{:S(2)}) collective-permute-start(bf16[128,2048]{1,0:T(8,128)(2,1)S(1)} %get-tuple-element.118), channel_id=1, source_target_pairs={{0,1},{1,0},{2,3},{3,2},{4,5},{5,4},{6,7},{7,6},{8,9},{9,8},{10,11... | collective-permute-start | bytes 1572872 | tf_op jit(solution)/shard_map/cond/branch_0_fun/ppermute | solution.py:511
  99.4 3.4 %collective-permute-start.5 = (bf16[128,2048]{1,0:T(8,128)(2,1)S(1)}, bf16[128,2048]{1,0:T(8,128)(2,1)S(1)}, u32[]{:S(2)}, u32[]{:S(2)}) collective-permute-start(bf16[128,2048]{1,0:T(8,128)(2,1)S(1)} %unpack_rows.15), channel_id=1, source_target_pairs={{0,1},{1,0},{2,3},{3,2},{4,5},{5,4},{6,7},{7,6},{8,9},{9,8},{10,11... | collective-permute-start | bytes 1572872 | tf_op jit(solution)/shard_map/cond/branch_0_fun/ppermute | solution.py:516
  (7 other events, 68.9 us)
where the time goes:
time: 105 us
  starting transfers between devices  54.3 us (52%)
  Pallas kernels  29.2 us (28%)
  waiting for transfers between devices  18.4 us (18%)
  between operations  1.53 us (1%)
    ppermute x16, starting transfers between devices, to_next_section(): return lax.ppermute(block, ('pp', 'cp'), route)  34.4 us
    pallas_call x4, Pallas kernels, attend(): pl.pallas_call(kernel, in_specs=specs(pltpu.HBM, 1) + specs(pltpu.VMEM, 2...  14.2 us
    ppermute x16, waiting for transfers between devices, to_next_section(): return lax.ppermute(block, ('pp', 'cp'), route)  11.7 us
    ppermute x3, starting transfers between devices, deliver(): twins.append(lax.ppermute(send, 'tp', swap))  11.4 us
    pallas_call x5, Pallas kernels, unpack_rows(): pl.pallas_call(kernel, in_specs=in_specs, out_specs=out_specs, scratch_sh...  9.8 us
    ppermute x6, starting transfers between devices, to_partner(): return lax.ppermute(block, 'cp', [(i, i ^ mask) for i in range(size)])  8.39 us
    ppermute x6, waiting for transfers between devices, to_partner(): return lax.ppermute(block, 'cp', [(i, i ^ mask) for i in range(size)])  5.48 us
  transfers between devices with their start and end apart: 26, of which 6 were waited for; matrix products, arithmetic and copies ran while one was open for 0% of the time, Pallas kernels for 25%

commit v1 on v0

--- a/solution.py
+++ b/solution.py
@@ -9,6 +9,8 @@
 
 
 masked_score = -1e30
+
+STEP_HEADS = 8
 
 
 def shifted(block, axis, distance):
@@ -163,6 +165,14 @@
     return [pl.BlockSpec(memory_space=space)] * count
 
 
+def message_order(cycle_size):
+    return [0, 1, 2, 3][:cycle_size]
+
+
+def piece_order(cycle_size):
+    return [0, 3, 1, 2][:cycle_size]
+
+
 def make_ready(keys, values, pair_order, limits, route_rows, where, *, cycle_size, split_size, packed_rows):
     row_count, width = keys.shape
     sections = route_rows.shape[0]
@@ -184,24 +194,24 @@
         chips = r_ref[pl.ds(section, 1), :] // split_size
         rank = rank_in_row(chips)
         none = jnp.zeros((packed_rows, half), jnp.float32)
-        for mask in range(cycle_size):
+        for spot, mask in enumerate(message_order(cycle_size)):
             ids = lax.broadcasted_iota(jnp.int32, (packed_rows, row_count), 0)
             pick = jnp.logical_and(ids == rank, chips == (place ^ mask)).astype(jnp.float32)
             first, second = pick[:, :half], pick[:, half:]
-            rows = slice(mask * packed_rows, (mask + 1) * packed_rows)
-            later = slice(total + mask * packed_rows, total + (mask + 1) * packed_rows)
+            rows = slice(spot * packed_rows, (spot + 1) * packed_rows)
+            later = slice(total + spot * packed_rows, total + (spot + 1) * packed_rows)
             pack_ref[rows, :] = jnp.concatenate([first, none, second, none], axis=1).astype(jnp.bfloat16)
             pack_ref[later, :] = jnp.concatenate([none, first, none, second], axis=1).astype(jnp.bfloat16)
         own = order_ref[section, place]
         lane = lax.broadcasted_iota(jnp.int32, (half, 2 * half), 1) % half
         query_pos = jnp.where(lane < block_len, own, 2 * cycle_size - 2 - own) * block_len + lane
         down = lax.broadcasted_iota(jnp.int32, (half, 2 * half), 0)
-        for mask in range(cycle_size):
+        for spot, mask in enumerate(piece_order(cycle_size)):
             pair = order_ref[section, place ^ mask]
             key_pos = jnp.where(down < block_len, pair, 2 * cycle_size - 2 - pair) * block_len + down
             for seq in range(2):
                 allowed = jnp.logical_and(key_pos <= query_pos, key_pos < limit_ref[seq, section])
-                mask_ref[seq, mask * half : (mask + 1) * half, :] = allowed.astype(jnp.float32)
+                mask_ref[seq, spot * half : (spot + 1) * half, :] = allowed.astype(jnp.float32)
 
     return pl.pallas_call(
         kernel,
@@ -217,30 +227,6 @@
     )(where, pair_order, limits, keys, values, route_rows)
 
 
-def count_rows(route_rows, heads, *, cycle_size, split_size):
-    sections, row_count = route_rows.shape
-
-    def kernel(r_ref, *refs):
-        head_refs, most_ref = refs[: cycle_size - 1], refs[cycle_size - 1]
-        tables = [r_ref[...].astype(jnp.float32)]
-        tables += [ref[row_count : row_count + 16, 0:row_count].astype(jnp.float32)[0:sections] for ref in head_refs]
-        table = jnp.concatenate(tables, axis=0)
-        most = jnp.zeros((sections * cycle_size, 1), jnp.float32)
-        for chip in range(cycle_size):
-            low = chip * split_size
-            hits = jnp.logical_and(table >= low, table < low + split_size).astype(jnp.float32)
-            most = jnp.maximum(most, jnp.sum(hits, axis=1, keepdims=True))
-        most_ref[0] = jnp.max(most).astype(jnp.int32)
-
-    return pl.pallas_call(
-        kernel,
-        out_shape=jax.ShapeDtypeStruct((1,), jnp.int32),
-        in_specs=specs(pltpu.VMEM, cycle_size),
-        out_specs=specs(pltpu.SMEM, 1)[0],
-        name="count_rows",
-    )(route_rows, *[in_vmem(head) for head in heads])
-
-
 def make_unpack(route_rows, heads, where, *, cycle_size, split_size, packed_rows, capacity):
     sections, row_count = route_rows.shape
     slot_rows = cycle_size * capacity
@@ -250,7 +236,7 @@
         place, core = where_ref[1], where_ref[2]
         source = (where_ref[0] + sections - 1) % sections
         slots_ref[...] = jnp.zeros(slots_ref.shape, jnp.bfloat16)
-        for mask in range(cycle_size):
+        for spot, mask in enumerate(message_order(cycle_size)):
             if mask == 0:
                 targets = r_ref[pl.ds(source, 1), :]
             else:
@@ -264,7 +250,7 @@
             for step, which in enumerate((core, 1 - core)):
                 slotted = one_hot(slots, targets == place * split_size + which, capacity)
                 at = pl.ds(pl.multiple_of((place ^ mask) * capacity, capacity), capacity)
-                slots_ref[step, at, mask * packed_rows : (mask + 1) * packed_rows] = lax.dot_general(
+                slots_ref[step, at, spot * packed_rows : (spot + 1) * packed_rows] = lax.dot_general(
                     slotted, packed, (((1,), (1,)), ((), ())), preferred_element_type=jnp.float32
                 ).astype(jnp.bfloat16)
 
@@ -277,40 +263,54 @@
     )(where, route_rows, *[in_vmem(head) for head in heads])
 
 
-def attend(queries, pieces, pack, allow, group, *, cycle_size, group_size, packed_rows):
+def attend(queries, pieces, pack, allow, first, count, *, cycle_size, group_size, packed_rows, choose=None):
     row_count = queries.shape[0]
     half = row_count // 2
     total_rows = pack.shape[0] // 2
     stride = total_rows // cycle_size
-    width = group_size * HD
-    step_heads = min(8, group_size)
+    step_heads = min(STEP_HEADS, group_size)
     step_width = step_heads * HD
-    steps = group_size // step_heads
+    head_steps = group_size // step_heads
+    width = count * step_width
+    skipped = first % head_steps
+    key_heads = (skipped + count - 1) // head_steps + 1
     scale = HD ** (-0.5)
 
-    def kernel(q_hbm, pack_ref, allow_ref, *refs):
-        kv_refs, out_refs = refs[:cycle_size], refs[cycle_size : 2 * cycle_size]
-        q_ref, keys_ref, values_ref, sems = refs[2 * cycle_size :]
-        for step in range(steps):
-            at = group * width + step * step_width
-            pltpu.make_async_copy(q_hbm.at[:, at : at + step_width], q_ref.at[step], sems.at[step]).start()
+    def kernel(*refs):
+        refs = list(refs)
+        q_hbm, pack_ref, allow_ref = refs[:3]
+        kv_refs = refs[3 : 3 + cycle_size]
+        refs = refs[3 + cycle_size :]
+        count_refs = (refs.pop(0), kv_refs[1:], refs.pop(0)) if choose else None
+        out_refs, refs = refs[:cycle_size], refs[cycle_size:]
+        keys_ref, values_ref, q_ref, sem = refs
+        at = slice(first * step_width, first * step_width + width)
+        load = pltpu.make_async_copy(q_hbm.at[:, at], q_ref, sem)
+        load.start()
 
         seq_rows = [slice(seq * half, (seq + 1) * half) for seq in range(2)]
         for seq in range(2):
             for mask, (_, key_col, value_col) in enumerate(pieces):
                 at = slice(mask * half, (mask + 1) * half)
-                keys_ref[seq, at, :] = kv_refs[mask][seq_rows[seq], key_col : key_col + HD]
-                values_ref[seq, :, at] = jnp.transpose(kv_refs[mask][seq_rows[seq], value_col : value_col + HD])
+                for head in range(key_heads):
+                    key_cols = slice(key_col + head * HD, key_col + (head + 1) * HD)
+                    value_cols = slice(value_col + head * HD, value_col + (head + 1) * HD)
+                    keys_ref[head, seq, at, :] = kv_refs[mask][seq_rows[seq], key_cols]
+                    values_ref[head, seq, :, at] = jnp.transpose(kv_refs[mask][seq_rows[seq], value_cols])
+
+        if choose:
+            count_too_low(*count_refs)
+        load.wait()
 
         def advance(step, carry):
-            pltpu.make_async_copy(q_hbm.at[:, 0:step_width], q_ref.at[step], sems.at[step]).wait()
+            cols = [
+                pl.ds(pl.multiple_of(step * step_width + h * HD, HD), HD) for h in range(step_heads)
+            ]
             attended = []
             for seq in range(2):
-                q = jnp.concatenate(
-                    [q_ref[step, seq_rows[seq], h * HD : (h + 1) * HD] for h in range(step_heads)], axis=0
-                )
+                q = jnp.concatenate([q_ref[seq_rows[seq], col] for col in cols], axis=0)
                 scores = lax.dot_general(
-                    keys_ref[seq], q, (((1,), (1,)), ((), ())), preferred_element_type=jnp.float32
+                    keys_ref[(step + skipped) // head_steps, seq], q, (((1,), (1,)), ((), ())), preferred_element_type=jnp.float32
                 )
                 tiles, totals = [], []
                 for pair in range(step_heads // 2):
@@ -321,46 +321,70 @@
                     tiles.append(block.astype(jnp.bfloat16))
                 weights = jnp.concatenate(tiles, axis=1)
                 total = jnp.concatenate(totals, axis=1)
-                summed = jnp.dot(values_ref[seq], weights, preferred_element_type=jnp.float32)
+                summed = jnp.dot(values_ref[(step + skipped) // head_steps, seq], weights, preferred_element_type=jnp.float32)
                 attended.append((summed / total).astype(jnp.bfloat16))
             for pair in range(step_heads // 2):
-                cols = slice(pair * 2 * half, (pair + 1) * 2 * half)
-                both = jnp.concatenate([attended[0][:, cols], attended[1][:, cols]], axis=1)
+                tile = slice(pair * 2 * half, (pair + 1) * 2 * half)
+                both = jnp.concatenate([attended[0][:, tile], attended[1][:, tile]], axis=1)
                 packed = lax.dot_general(
                     pack_ref[...], both, (((1,), (1,)), ((), ())), preferred_element_type=jnp.float32
                 ).astype(jnp.bfloat16)
                 for which in range(2):
                     head = pl.ds(pl.multiple_of(step * step_width + (2 * pair + which) * HD, HD), HD)
-                    for mask in range(cycle_size):
-                        at = which * total_rows + mask * stride
-                        out_refs[mask][:, head] = packed[at : at + packed_rows]
+                    for spot in range(cycle_size):
+                        at = which * total_rows + spot * stride
+                        out_refs[spot][:, head] = packed[at : at + packed_rows]
             return carry
 
-        lax.fori_loop(0, steps, advance, 0)
-
+        lax.fori_loop(0, count, advance, 0)
+
+    def count_too_low(routes_ref, head_refs, count_ref):
+        sections = routes_ref.shape[0]
+        _, heights, cores = choose
+        tables = [routes_ref[...].astype(jnp.float32)]
+        tables += [ref[row_count : row_count + 16, 0:row_count].astype(jnp.float32)[0:sections] for ref in head_refs]
+        table = jnp.concatenate(tables, axis=0)
+        most = jnp.zeros((sections * cycle_size, 1), jnp.float32)
+        for low in range(0, cycle_size * cores, cores):
+            hits = jnp.logical_and(table >= low, table < low + cores).astype(jnp.float32)
+            most = jnp.maximum(most, jnp.sum(hits, axis=1, keepdims=True))
+        most = jnp.max(most).astype(jnp.int32)
+        count_ref[0] = sum((most > height).astype(jnp.int32) for height in heights)
+
+    args = [queries]
+    args += [in_vmem(array) for array in [pack, allow] + [piece[0] for piece in pieces]]
+    in_specs = specs(pltpu.HBM, 1) + specs(pltpu.VMEM, 2 + cycle_size)
+    out_specs, out_shape = specs(pltpu.VMEM, cycle_size), [pltpu.VMEM((packed_rows, width), jnp.bfloat16)] * cycle_size
+    scratch = [
+        pltpu.VMEM((key_heads, 2, cycle_size * half, HD), jnp.bfloat16),
+        pltpu.VMEM((key_heads, 2, HD, cycle_size * half), jnp.bfloat16),
+        pltpu.VMEM((row_count, width), jnp.bfloat16),
+        pltpu.SemaphoreType.DMA(()),
+    ]
+    if choose:
+        args.append(choose[0])
+        in_specs += specs(pltpu.VMEM, 1)
+        out_specs = specs(pltpu.SMEM, 1) + out_specs
+        out_shape = [jax.ShapeDtypeStruct((1,), jnp.int32)] + out_shape
+    estimate = pl.CostEstimate(flops=20000000000, transcendentals=0, bytes_accessed=0) if choose else None
     return pl.pallas_call(
         kernel,
-        in_specs=specs(pltpu.HBM, 1) + specs(pltpu.VMEM, 2 + cycle_size),
-        out_specs=specs(pltpu.VMEM, cycle_size),
-        out_shape=[pltpu.VMEM((packed_rows, width), jnp.bfloat16)] * cycle_size,
-        scratch_shapes=[
-            pltpu.VMEM((steps, row_count, step_width), jnp.bfloat16),
-            pltpu.VMEM((2, cycle_size * half, HD), jnp.bfloat16),
-            pltpu.VMEM((2, HD, cycle_size * half), jnp.bfloat16),
-            pltpu.SemaphoreType.DMA((steps,)),
-        ],
+        in_specs=in_specs,
+        out_specs=out_specs,
+        out_shape=out_shape,
+        scratch_shapes=scratch,
         compiler_params=pltpu.CompilerParams(vmem_limit_bytes=8 * 1024 * 1024),
-        cost_estimate=pl.CostEstimate(flops=20000000000, transcendentals=0, bytes_accessed=0) if group == 0 else None,
+        cost_estimate=estimate,
         name="attend",
-    )(queries, in_vmem(pack), in_vmem(allow), *[in_vmem(piece[0]) for piece in pieces])
-
-
-def unpack_rows(received, slots, where, out, group, twins, *, group_count, own, twin):
+    )(*args)
+
+
+def unpack_rows(received, slots, where, out, first, twins, *, half_width, own, twin):
     cycle_size = len(received)
     packed_rows, width = received[0].shape
     rows = slots.shape[1]
     spare = slots.shape[2] // cycle_size - packed_rows
-    full = 2 * group_count * width
+    full = 2 * half_width
     tile = 512
     steps = width // tile
 
@@ -376,17 +400,16 @@
         send_ref = refs.pop(0) if twin else None
         own_ref, sems = refs if own else (None, None)
 
-        def columns(which, index, step, size):
-            at = (which * group_count + index) * width + step * size
-            return pl.ds(pl.multiple_of(at, size), size)
+        def columns(which, column, size):
+            return pl.ds(pl.multiple_of(which * half_width + column, tile), size)
 
         def copy(step):
             cols = pl.ds(pl.multiple_of(step * tile, tile), tile)
-            at = columns(where_ref[2], group, step, tile)
+            at = columns(where_ref[2], first + step * tile, tile)
             return pltpu.make_async_copy(own_ref.at[:, cols], out_ref.at[:, at], sems.at[step])
 
         def copy_twin(index):
-            at = columns(1 - where_ref[2], index, 0, width)
+            at = columns(1 - where_ref[2], twins[index][1], twin_refs[index].shape[1])
             return pltpu.make_async_copy(twin_refs[index], out_ref.at[:, at], sems.at[steps + index])
 
         def advance(step, carry):
@@ -420,7 +443,7 @@
         in_specs += specs(pltpu.SMEM, 1)
         args.append(where)
     in_specs += specs(pltpu.VMEM, cycle_size + 1 + len(twins))
-    args += [in_vmem(block) for block in list(received) + [slots] + list(twins)]
+    args += [in_vmem(block) for block in list(received) + [slots] + [block for block, _ in twins]]
     if own:
         if out is not None:
             in_specs += specs(pl.ANY, 1)
@@ -447,11 +470,11 @@
     )(*args)
 
 
-def place_twin(block, out, where, group, *, group_count):
+def place_twin(block, out, where, first, *, half_width):
     width = block.shape[1]
 
     def kernel(where_ref, in_ref, old_ref, out_ref, sem):
-        at = pl.multiple_of(((1 - where_ref[2]) * group_count + group) * width, width)
+        at = pl.multiple_of((1 - where_ref[2]) * half_width + first, HD)
         copy = pltpu.make_async_copy(in_ref, out_ref.at[:, pl.ds(at, width)], sem)
         copy.start()
         copy.wait()
@@ -477,52 +500,64 @@
     dest_count = cycle_size * split_size
     capacity = 2 * row_count // dest_count
     most_rows = min(row_count, split_size * capacity)
-    masks = [2, 3, 1, 0]
     where = jnp.stack([lax.axis_index("pp"), lax.axis_index("cp"), lax.axis_index("tp")]).astype(jnp.int32)
     route_rows = routes[:, :, 0]
     sizes = dict(cycle_size=cycle_size, split_size=split_size, packed_rows=most_rows)
     heads_of = dict(cycle_size=cycle_size, group_size=group_size)
     head, rest, pack, allow = make_ready(keys, values, pair_order, lengths.T, route_rows, where, **sizes)
-    heads = [head] + [to_partner(head, mask) for mask in range(1, cycle_size)]
+    head_steps = group_size // min(STEP_HEADS, group_size)
+    counts = [head_steps] * group_count
+    chunks = [(sum(counts[:at]), count) for at, count in enumerate(counts)]
+    heads = {mask: to_partner(head, mask) for mask in range(1, cycle_size)}
+    heads[0] = head
     rests = [rest] + [to_partner(rest, mask) for mask in (1, 2)]
-    most = count_rows(route_rows, heads[1:], cycle_size=cycle_size, split_size=split_size)
-    pieces = [(piece, 0, HD) for piece in heads]
-    leading = attend(queries, pieces, pack, allow, 0, packed_rows=most_rows, **heads_of)
-
-    def deliver(packed_rows, queries, pack, allow, route_rows, where, heads, rests, leading):
+    heights = [most_rows * 3 // 4, most_rows * 7 // 8, most_rows]
+    choice, *leading = attend(
+        queries,
+        [(heads[mask], 0, HD) for mask in piece_order(cycle_size)],
+        pack,
+        allow,
+        *chunks[0],
+        packed_rows=most_rows,
+        choose=(route_rows, heights[:-1], split_size),
+        **heads_of,
+    )
+    heads = [heads[mask] for mask in range(1, cycle_size)]
+    def deliver(packed_rows, queries, pack, allow, route_rows, where, head, heads, rests, leading):
         rests = rests + [to_partner(rests[2], 1)]
         arrived = []
-        for group in range(group_count):
-            if group == 0:
+        every = [head] + list(heads)
+        for first, count in chunks:
+            if first == 0:
                 packed = [block[:packed_rows] for block in leading]
             else:
-                first = (group - 1) * HD
-                pieces = [(piece, first, first + keys.shape[1] - HD) for piece in rests]
-                packed = attend(queries, pieces, pack, allow, group, packed_rows=packed_rows, **heads_of)
-            sent = {mask: to_next_section(packed[mask], mask) for mask in masks}
-            arrived.append([sent[mask] for mask in range(cycle_size)])
+                key_col = (first // head_steps - 1) * HD
+                value_col = key_col + keys.shape[1] - HD
+                pieces = [(rests[mask], key_col, value_col) for mask in piece_order(cycle_size)]
+                if first < head_steps:
+                    pieces = [(every[mask], 0, HD) for mask in piece_order(cycle_size)]
+                packed = attend(queries, pieces, pack, allow, first, count, packed_rows=packed_rows, **heads_of)
+            arrived.append([to_next_section(*sent) for sent in zip(packed, message_order(cycle_size))])
         slots = make_unpack(route_rows, heads, where, capacity=capacity, **sizes)
         out, twins = None, []
         swap = [(0, 1), (1, 0)]
-        for group in range(group_count - 1):
+        starts = [first * width // (group_count * head_steps) for first, _ in chunks]
+        for received, column in list(zip(arrived, starts))[:-1]:
             out, send = unpack_rows(
-                arrived[group], slots, where, out, group, [], group_count=group_count, own=True, twin=True
+                received, slots, where, out, column, [], half_width=width, own=True, twin=True
             )
-            twins.append(lax.ppermute(send, "tp", swap))
-        last = group_count - 1
+            twins.append((lax.ppermute(send, "tp", swap), column))
         (send,) = unpack_rows(
-            arrived[last], slots, where, None, last, [], group_count=group_count, own=False, twin=True
+            arrived[-1], slots, where, None, starts[-1], [], half_width=width, own=False, twin=True
         )
         late = lax.ppermute(send, "tp", swap)
         (out,) = unpack_rows(
-            arrived[last], slots, where, out, last, twins, group_count=group_count, own=True, twin=False
-        )
-        return place_twin(late, out, where, last, group_count=group_count)
-
-    heights = [most_rows * 3 // 4, most_rows * 7 // 8, most_rows]
-    choice = sum((most[0] > height).astype(jnp.int32) for height in heights[:-1])
+            arrived[-1], slots, where, out, starts[-1], twins, half_width=width, own=True, twin=False
+        )
+        return place_twin(late, out, where, starts[-1], half_width=width)
+
     branches = [lambda *args, height=height: deliver(height, *args) for height in heights]
-    return lax.switch(choice, branches, queries, pack, allow, route_rows, where, heads[1:], rests, leading)
+    return lax.switch(choice[0], branches, queries, pack, allow, route_rows, where, head, heads, rests, leading)
 
 
 def solution(mesh):

time: 105 us -> 115 us (1.095)
  the two profiles are of different devices: /device:TPU:7 before, /device:TPU:0 now
where the time goes in v1:
time: 115 us; the launch traced here: 113 us
  starting transfers between devices  55.5 us (48%)
  Pallas kernels  28.5 us (25%)
  waiting for transfers between devices  24.4 us (21%)
  local copies, waits for them, and re-layouts  3.06 us (3%)
    ppermute x16, starting transfers between devices, to_next_section(): return lax.ppermute(block, ('pp', 'cp'), route)  44.6 us
    ppermute x16, waiting for transfers between devices, to_next_section(): return lax.ppermute(block, ('pp', 'cp'), route)  16.6 us
    pallas_call x4, Pallas kernels, attend(): pl.pallas_call(kernel, in_specs=in_specs, out_specs=out_specs, out_shape=...  15.2 us
    ppermute x6, starting transfers between devices, to_partner(): return lax.ppermute(block, 'cp', [(i, i ^ mask) for i in range(size)])  10.1 us
    pallas_call x5, Pallas kernels, unpack_rows(): pl.pallas_call(kernel, in_specs=in_specs, out_specs=out_specs, scratch_sh...  9.64 us
    ppermute x6, waiting for transfers between devices, to_partner(): return lax.ppermute(block, 'cp', [(i, i ^ mask) for i in range(size)])  7.88 us
    cond x12, local copies, waits for them, and re-layouts  2.99 us
  transfers between devices with their start and end apart: 26, of which 7 were waited for; matrix products, arithmetic and copies ran while one was open for 0% of the time, Pallas kernels for 23%

profile of v1, /device:TPU:0, one launch (start us, length us, event | category | flops | bytes accessed | tf_op | source)
XLA Modules:
  0.0 113.2 jit_solution(2835777259559634704)
XLA Ops:
  1.3 5.1 %collective-permute-start.63 = (bf16[144,256]{1,0:T(8,128)(2,1)S(1)}, bf16[144,256]{1,0:T(8,128)(2,1)S(1)}, u32[]{:S(2)}, u32[]{:S(2)}) collective-permute-start(bf16[144,256]{1,0:T(8,128)(2,1)S(1)} %get-tuple-element.209.refs_3_), channel_id=1, source_target_pairs={{0,6},{2,4},{4,2},{6,0},{1,7},{3,5},{5,3},{7,1},{8,14},{10,12},{12... | collective-permute-start | bytes 221192 | tf_op jit(solution)/shard_map/ppermute | solution.py:127
  7.0 2.3 %collective-permute-start.66 = (bf16[128,768]{1,0:T(8,128)(2,1)S(1)}, bf16[128,768]{1,0:T(8,128)(2,1)S(1)}, u32[]{:S(2)}, u32[]{:S(2)}) collective-permute-start(bf16[128,768]{1,0:T(8,128)(2,1)S(1)} %get-tuple-element.211), channel_id=1, source_target_pairs={{0,4},{2,6},{4,0},{6,2},{1,5},{3,7},{5,1},{7,3},{8,12},{10,14},{12... | collective-permute-start | bytes 589832 | tf_op jit(solution)/shard_map/ppermute | solution.py:127
  9.3 2.0 %collective-permute-start.67 = (bf16[128,768]{1,0:T(8,128)(2,1)S(1)}, bf16[128,768]{1,0:T(8,128)(2,1)S(1)}, u32[]{:S(2)}, u32[]{:S(2)}) collective-permute-start(bf16[128,768]{1,0:T(8,128)(2,1)S(1)} %get-tuple-element.211), channel_id=1, source_target_pairs={{0,2},{2,0},{4,6},{6,4},{1,3},{3,1},{5,7},{7,5},{8,10},{10,8},{12,... | collective-permute-start | bytes 589832 | tf_op jit(solution)/shard_map/ppermute | solution.py:127
  12.4 5.7 %collective-permute-done.65.refs_6_ = bf16[144,256]{1,0:T(8,128)(2,1)S(1)} collective-permute-done((bf16[144,256]{1,0:T(8,128)(2,1)S(1)}, bf16[144,256]{1,0:T(8,128)(2,1)S(1)}, u32[]{:S(2)}, u32[]{:S(2)}) %collective-permute-start.65) | collective-permute-done | bytes 73760 | tf_op jit(solution)/shard_map/ppermute | solution.py:127
  18.1 5.0 %attend.19 = (s32[1]{0:T(128)}, bf16[64,2048]{1,0:T(8,128)(2,1)S(1)}, bf16[64,2048]{1,0:T(8,128)(2,1)S(1)}, bf16[64,2048]{1,0:T(8,128)(2,1)S(1)}, bf16[64,2048]{1,0:T(8,128)(2,1)S(1)}) custom-call(bf16[128,8192]{1,0:T(8,128)(2,1)} %refs_0_.1, bf16[512,256]{1,0:T(8,128)(2,1)S(1)} %get-tuple-element.207.refs_1_, ...), custom_call_target="tpu_custom_call" | custom-call | flops 20000000000 | tf_op jit(solution)/shard_map/attend/pallas_call | solution.py:370
  23.8 89.2 %conditional.1 = (bf16[128,16384]{1,0:T(8,128)(2,1)}) conditional(s32[]{:T(128)} %bitcast.5, (bf16[128,768]{1,0:T(8,128)(2,1)S(1)}, bf16[128,8192]{1,0:T(8,128)(2,1)S(1)}, bf16[512,256]{1,0:T(8,128)(2,1)S(1)}, f32[2,256,128]{2,1,0:T(8,128)S(1)}, bf16[128,768]{1,0:T(8,128)(2,1)S(1)}, /*index=5*/bf16[128,768]{1,0:T(8,128)(2,1)S(1)}, ...), branch_computations={%region_0.0_spmd, %region_1.0_spmd, %region_2.0_spmd} | conditional | bytes 51119208 | solution.py:560
  23.9 1.5 %collective-permute-start.27 = (bf16[56,2048]{1,0:T(8,128)(2,1)S(1)}, bf16[56,2048]{1,0:T(8,128)(2,1)S(1)}, u32[]{:S(2)}, u32[]{:S(2)}) collective-permute-start(bf16[56,2048]{1,0:T(8,128)(2,1)S(1)} %slice.20), channel_id=1, source_target_pairs={{0,8},{2,10},{4,12},{6,14},{8,16},{10,18},{12,20},{14,22},{16,24},... | collective-permute-start | bytes 688136 | tf_op jit(solution)/shard_map/cond/branch_1_fun/ppermute | solution.py:137
  25.5 3.0 %collective-permute-start.28 = (bf16[56,2048]{1,0:T(8,128)(2,1)S(1)}, bf16[56,2048]{1,0:T(8,128)(2,1)S(1)}, u32[]{:S(2)}, u32[]{:S(2)}) collective-permute-start(bf16[56,2048]{1,0:T(8,128)(2,1)S(1)} %slice.21), channel_id=1, source_target_pairs={{0,10},{2,8},{4,14},{6,12},{8,18},{10,16},{12,22},{14,20},{16,26},... | collective-permute-start | bytes 688136 | tf_op jit(solution)/shard_map/cond/branch_1_fun/ppermute | solution.py:137
  29.7 2.2 %collective-permute-start.30 = (bf16[56,2048]{1,0:T(8,128)(2,1)S(1)}, bf16[56,2048]{1,0:T(8,128)(2,1)S(1)}, u32[]{:S(2)}, u32[]{:S(2)}) collective-permute-start(bf16[56,2048]{1,0:T(8,128)(2,1)S(1)} %slice.23), channel_id=1, source_target_pairs={{0,14},{2,12},{4,10},{6,8},{8,22},{10,20},{12,18},{14,16},{16,30},... | collective-permute-start | bytes 688136 | tf_op jit(solution)/shard_map/cond/branch_1_fun/ppermute | solution.py:137
  33.0 2.9 %attend.14 = (bf16[56,2048]{1,0:T(8,128)(2,1)S(1)}, bf16[56,2048]{1,0:T(8,128)(2,1)S(1)}, bf16[56,2048]{1,0:T(8,128)(2,1)S(1)}, bf16[56,2048]{1,0:T(8,128)(2,1)S(1)}) custom-call(bf16[128,8192]{1,0:T(8,128)(2,1)S(1)} %get-tuple-element.133.refs_0_, bf16[512,256]{1,0:T(8,128)(2,1)S(1)} %get-tuple-element.134.refs_1_, ...), custom_call_target="tpu_custom_call" | custom-call | tf_op jit(solution)/shard_map/cond/branch_1_fun/attend/pallas_call | solution.py:370
  35.9 1.5 %collective-permute-start.32 = (bf16[56,2048]{1,0:T(8,128)(2,1)S(1)}, bf16[56,2048]{1,0:T(8,128)(2,1)S(1)}, u32[]{:S(2)}, u32[]{:S(2)}) collective-permute-start(bf16[56,2048]{1,0:T(8,128)(2,1)S(1)} %get-tuple-element.152), channel_id=1, source_target_pairs={{0,8},{2,10},{4,12},{6,14},{8,16},{10,18},{12,20},{14,22},{16,24},... | collective-permute-start | bytes 688136 | tf_op jit(solution)/shard_map/cond/branch_1_fun/ppermute | solution.py:137
  37.4 3.7 %collective-permute-done.27.refs_1_ = bf16[56,2048]{1,0:T(8,128)(2,1)S(1)} collective-permute-done((bf16[56,2048]{1,0:T(8,128)(2,1)S(1)}, bf16[56,2048]{1,0:T(8,128)(2,1)S(1)}, u32[]{:S(2)}, u32[]{:S(2)}) %collective-permute-start.27) | collective-permute-done | bytes 229408 | tf_op jit(solution)/shard_map/cond/branch_1_fun/ppermute | solution.py:137
  41.1 3.6 %attend.15 = (bf16[56,2048]{1,0:T(8,128)(2,1)S(1)}, bf16[56,2048]{1,0:T(8,128)(2,1)S(1)}, bf16[56,2048]{1,0:T(8,128)(2,1)S(1)}, bf16[56,2048]{1,0:T(8,128)(2,1)}) custom-call(bf16[128,8192]{1,0:T(8,128)(2,1)S(1)} %get-tuple-element.133.refs_0_, bf16[512,256]{1,0:T(8,128)(2,1)S(1)} %get-tuple-element.134.refs_1_, ...), custom_call_target="tpu_custom_call" | custom-call | tf_op jit(solution)/shard_map/cond/branch_1_fun/attend/pallas_call | solution.py:370
  44.7 12.4 %collective-permute-start.34 = (bf16[56,2048]{1,0:T(8,128)(2,1)S(1)}, bf16[56,2048]{1,0:T(8,128)(2,1)S(1)}, u32[]{:S(2)}, u32[]{:S(2)}) collective-permute-start(bf16[56,2048]{1,0:T(8,128)(2,1)S(1)} %get-tuple-element.154), channel_id=1, source_target_pairs={{0,12},{2,14},{4,8},{6,10},{8,20},{10,22},{12,16},{14,18},{16,28},... | collective-permute-start | bytes 688136 | tf_op jit(solution)/shard_map/cond/branch_1_fun/ppermute | solution.py:137
  59.6 8.4 %collective-permute-start.39 = (bf16[56,2048]{1,0:T(8,128)(2,1)S(1)}, bf16[56,2048]{1,0:T(8,128)(2,1)S(1)}, u32[]{:S(2)}, u32[]{:S(2)}) collective-permute-start(bf16[56,2048]{1,0:T(8,128)(2,1)S(1)} %get-tuple-element.160), channel_id=1, source_target_pairs={{0,12},{2,14},{4,8},{6,10},{8,20},{10,22},{12,16},{14,18},{16,28},... | collective-permute-start | bytes 688136 | tf_op jit(solution)/shard_map/cond/branch_1_fun/ppermute | solution.py:137
  68.0 3.8 %attend.13 = (bf16[56,2048]{1,0:T(8,128)(2,1)}, bf16[56,2048]{1,0:T(8,128)(2,1)}, bf16[56,2048]{1,0:T(8,128)(2,1)}, bf16[56,2048]{1,0:T(8,128)(2,1)}) custom-call(bf16[128,8192]{1,0:T(8,128)(2,1)S(1)} %get-tuple-element.133.refs_0_, bf16[512,256]{1,0:T(8,128)(2,1)S(1)} %get-tuple-element.134.refs_1_, f32[2,256,128]{2,1,0:T(8,128)S(1)} %get-tuple-element.135.refs_2_, ...), custom_call_target="tpu_custom_call" | custom-call | tf_op jit(solution)/shard_map/cond/branch_1_fun/attend/pallas_call | solution.py:370
  72.5 5.8 %collective-permute-start.22 = (bf16[56,2048]{1,0:T(8,128)(2,1)}, bf16[56,2048]{1,0:T(8,128)(2,1)S(1)}, u32[]{:S(2)}, u32[]{:S(2)}) collective-permute-start(bf16[56,2048]{1,0:T(8,128)(2,1)} %get-tuple-element.139), channel_id=1, source_target_pairs={{0,8},{2,10},{4,12},{6,14},{8,16},{10,18},{12,20},{14,22},{16,24},... | collective-permute-start | bytes 688136 | tf_op jit(solution)/shard_map/cond/branch_1_fun/ppermute | solution.py:137
  78.3 7.6 %collective-permute-done.37.refs_1_ = bf16[56,2048]{1,0:T(8,128)(2,1)S(1)} collective-permute-done((bf16[56,2048]{1,0:T(8,128)(2,1)S(1)}, bf16[56,2048]{1,0:T(8,128)(2,1)S(1)}, u32[]{:S(2)}, u32[]{:S(2)}) %collective-permute-start.37) | collective-permute-done | bytes 229408 | tf_op jit(solution)/shard_map/cond/branch_1_fun/ppermute | solution.py:137
  85.8 5.4 %collective-permute-start.23 = (bf16[56,2048]{1,0:T(8,128)(2,1)}, bf16[56,2048]{1,0:T(8,128)(2,1)S(1)}, u32[]{:S(2)}, u32[]{:S(2)}) collective-permute-start(bf16[56,2048]{1,0:T(8,128)(2,1)} %get-tuple-element.140), channel_id=1, source_target_pairs={{0,10},{2,8},{4,14},{6,12},{8,18},{10,16},{12,22},{14,20},{16,26},... | collective-permute-start | bytes 688136 | tf_op jit(solution)/shard_map/cond/branch_1_fun/ppermute | solution.py:137
  95.6 2.1 %unpack_rows.21 = (bf16[128,16384]{1,0:T(8,128)(2,1)}, bf16[128,2048]{1,0:T(8,128)(2,1)S(1)}) custom-call(s32[3]{0:T(128)S(1)} %get-tuple-element.132.where_ref.refs_0_, bf16[56,2048]{1,0:T(8,128)(2,1)S(1)} %collective-permute-done.27.refs_1_, bf16[56,2048]{1,0:T(8,128)(2,1)S(1)} %collective-permute-done.28.refs_2_, ...), custom_call_target="tpu_custom_call" | custom-call | tf_op jit(solution)/shard_map/cond/branch_1_fun/unpack_rows/pallas_call | solution.py:461
  98.7 2.1 %unpack_rows.22 = (bf16[128,16384]{1,0:T(8,128)(2,1)}, bf16[128,2048]{1,0:T(8,128)(2,1)S(1)}) custom-call(s32[3]{0:T(128)S(1)} %get-tuple-element.132.where_ref.refs_0_, bf16[56,2048]{1,0:T(8,128)(2,1)S(1)} %collective-permute-done.32.refs_1_, bf16[56,2048]{1,0:T(8,128)(2,1)S(1)} %collective-permute-done.33.refs_2_, ...), custom_call_target="tpu_custom_call", output_to_operand_aliasing={{0}: (6, {})} | custom-call | tf_op jit(solution)/shard_map/cond/branch_1_fun/unpack_rows/pallas_call | solution.py:461
  100.9 2.6 %unpack_rows.23 = (bf16[128,16384]{1,0:T(8,128)(2,1)}, bf16[128,2048]{1,0:T(8,128)(2,1)S(1)}) custom-call(s32[3]{0:T(128)S(1)} %get-tuple-element.132.where_ref.refs_0_, bf16[56,2048]{1,0:T(8,128)(2,1)S(1)} %collective-permute-done.37.refs_1_, bf16[56,2048]{1,0:T(8,128)(2,1)S(1)} %copy-done.11, ...), custom_call_target="tpu_custom_call", output_to_operand_aliasing={{0}: (6, {})} | custom-call | tf_op jit(solution)/shard_map/cond/branch_1_fun/unpack_rows/pallas_call | solution.py:461
  104.1 4.1 %collective-permute-done.24.refs_2_.refs_3_ = bf16[56,2048]{1,0:T(8,128)(2,1)S(1)} collective-permute-done((bf16[56,2048]{1,0:T(8,128)(2,1)}, bf16[56,2048]{1,0:T(8,128)(2,1)S(1)}, u32[]{:S(2)}, u32[]{:S(2)}) %collective-permute-start.24) | collective-permute-done | bytes 229408 | tf_op jit(solution)/shard_map/cond/branch_1_fun/ppermute | solution.py:137
  109.1 2.1 %unpack_rows.24.old_ref = bf16[128,16384]{1,0:T(8,128)(2,1)} custom-call(s32[3]{0:T(128)S(1)} %get-tuple-element.132.where_ref.refs_0_, bf16[56,2048]{1,0:T(8,128)(2,1)S(1)} %collective-permute-done.22.refs_0_.refs_1_, bf16[56,2048]{1,0:T(8,128)(2,1)S(1)} %collective-permute-done.23.refs_1_.refs_2_, ...), custom_call_target="tpu_custom_call", output_to_operand_aliasing={{}: (9, {})} | custom-call | tf_op jit(solution)/shard_map/cond/branch_1_fun/unpack_rows/pallas_call | solution.py:461
  (62 shorter events, 16.7 us)
Async XLA Ops:
  1.3 10.1 %collective-permute-start.63 = (bf16[144,256]{1,0:T(8,128)(2,1)S(1)}, bf16[144,256]{1,0:T(8,128)(2,1)S(1)}, u32[]{:S(2)}, u32[]{:S(2)}) collective-permute-start(bf16[144,256]{1,0:T(8,128)(2,1)S(1)} %get-tuple-element.209.refs_3_), channel_id=1, source_target_pairs={{0,6},{2,4},{4,2},{6,0},{1,7},{3,5},{5,3},{7,1},{8,14},{10,12},{12... | collective-permute-start | bytes 221192 | tf_op jit(solution)/shard_map/ppermute | solution.py:127
  6.4 6.0 %collective-permute-start.64 = (bf16[144,256]{1,0:T(8,128)(2,1)S(1)}, bf16[144,256]{1,0:T(8,128)(2,1)S(1)}, u32[]{:S(2)}, u32[]{:S(2)}) collective-permute-start(bf16[144,256]{1,0:T(8,128)(2,1)S(1)} %get-tuple-element.209.refs_3_), channel_id=1, source_target_pairs={{0,2},{2,0},{4,6},{6,4},{1,3},{3,1},{5,7},{7,5},{8,10},{10,8},{12,... | collective-permute-start | bytes 221192 | tf_op jit(solution)/shard_map/ppermute | solution.py:127
  6.4 11.7 %collective-permute-start.65 = (bf16[144,256]{1,0:T(8,128)(2,1)S(1)}, bf16[144,256]{1,0:T(8,128)(2,1)S(1)}, u32[]{:S(2)}, u32[]{:S(2)}) collective-permute-start(bf16[144,256]{1,0:T(8,128)(2,1)S(1)} %get-tuple-element.209.refs_3_), channel_id=1, source_target_pairs={{0,4},{2,6},{4,0},{6,2},{1,5},{3,7},{5,1},{7,3},{8,12},{10,14},{12... | collective-permute-start | bytes 221192 | tf_op jit(solution)/shard_map/ppermute | solution.py:127
  7.0 16.8 %collective-permute-start.66 = (bf16[128,768]{1,0:T(8,128)(2,1)S(1)}, bf16[128,768]{1,0:T(8,128)(2,1)S(1)}, u32[]{:S(2)}, u32[]{:S(2)}) collective-permute-start(bf16[128,768]{1,0:T(8,128)(2,1)S(1)} %get-tuple-element.211), channel_id=1, source_target_pairs={{0,4},{2,6},{4,0},{6,2},{1,5},{3,7},{5,1},{7,3},{8,12},{10,14},{12... | collective-permute-start | bytes 589832 | tf_op jit(solution)/shard_map/ppermute | solution.py:127
  9.3 14.5 %collective-permute-start.67 = (bf16[128,768]{1,0:T(8,128)(2,1)S(1)}, bf16[128,768]{1,0:T(8,128)(2,1)S(1)}, u32[]{:S(2)}, u32[]{:S(2)}) collective-permute-start(bf16[128,768]{1,0:T(8,128)(2,1)S(1)} %get-tuple-element.211), channel_id=1, source_target_pairs={{0,2},{2,0},{4,6},{6,4},{1,3},{3,1},{5,7},{7,5},{8,10},{10,8},{12,... | collective-permute-start | bytes 589832 | tf_op jit(solution)/shard_map/ppermute | solution.py:127
  23.9 17.2 %collective-permute-start.27 = (bf16[56,2048]{1,0:T(8,128)(2,1)S(1)}, bf16[56,2048]{1,0:T(8,128)(2,1)S(1)}, u32[]{:S(2)}, u32[]{:S(2)}) collective-permute-start(bf16[56,2048]{1,0:T(8,128)(2,1)S(1)} %slice.20), channel_id=1, source_target_pairs={{0,8},{2,10},{4,12},{6,14},{8,16},{10,18},{12,20},{14,22},{16,24},... | collective-permute-start | bytes 688136 | tf_op jit(solution)/shard_map/cond/branch_1_fun/ppermute | solution.py:137
  25.4 7.6 %collective-permute-start.21 = (bf16[128,768]{1,0:T(8,128)(2,1)S(1)}, bf16[128,768]{1,0:T(8,128)(2,1)S(1)}, u32[]{:S(2)}, u32[]{:S(2)}) collective-permute-start(bf16[128,768]{1,0:T(8,128)(2,1)S(1)} %get-tuple-element.137.refs_6_), channel_id=1, source_target_pairs={{0,2},{2,0},{4,6},{6,4},{1,3},{3,1},{5,7},{7,5},{8,10},{10,8},{12,... | collective-permute-start | bytes 589832 | tf_op jit(solution)/shard_map/cond/branch_1_fun/ppermute | solution.py:127
  25.5 19.2 %collective-permute-start.28 = (bf16[56,2048]{1,0:T(8,128)(2,1)S(1)}, bf16[56,2048]{1,0:T(8,128)(2,1)S(1)}, u32[]{:S(2)}, u32[]{:S(2)}) collective-permute-start(bf16[56,2048]{1,0:T(8,128)(2,1)S(1)} %slice.21), channel_id=1, source_target_pairs={{0,10},{2,8},{4,14},{6,12},{8,18},{10,16},{12,22},{14,20},{16,26},... | collective-permute-start | bytes 688136 | tf_op jit(solution)/shard_map/cond/branch_1_fun/ppermute | solution.py:137
  28.5 28.7 %collective-permute-start.29 = (bf16[56,2048]{1,0:T(8,128)(2,1)S(1)}, bf16[56,2048]{1,0:T(8,128)(2,1)S(1)}, u32[]{:S(2)}, u32[]{:S(2)}) collective-permute-start(bf16[56,2048]{1,0:T(8,128)(2,1)S(1)} %slice.22), channel_id=1, source_target_pairs={{0,12},{2,14},{4,8},{6,10},{8,20},{10,22},{12,16},{14,18},{16,28},... | collective-permute-start | bytes 688136 | tf_op jit(solution)/shard_map/cond/branch_1_fun/ppermute | solution.py:137
  29.7 27.4 %collective-permute-start.30 = (bf16[56,2048]{1,0:T(8,128)(2,1)S(1)}, bf16[56,2048]{1,0:T(8,128)(2,1)S(1)}, u32[]{:S(2)}, u32[]{:S(2)}) collective-permute-start(bf16[56,2048]{1,0:T(8,128)(2,1)S(1)} %slice.23), channel_id=1, source_target_pairs={{0,14},{2,12},{4,10},{6,8},{8,22},{10,20},{12,18},{14,16},{16,30},... | collective-permute-start | bytes 688136 | tf_op jit(solution)/shard_map/cond/branch_1_fun/ppermute | solution.py:137
  35.9 23.0 %collective-permute-start.32 = (bf16[56,2048]{1,0:T(8,128)(2,1)S(1)}, bf16[56,2048]{1,0:T(8,128)(2,1)S(1)}, u32[]{:S(2)}, u32[]{:S(2)}) collective-permute-start(bf16[56,2048]{1,0:T(8,128)(2,1)S(1)} %get-tuple-element.152), channel_id=1, source_target_pairs={{0,8},{2,10},{4,12},{6,14},{8,16},{10,18},{12,20},{14,22},{16,24},... | collective-permute-start | bytes 688136 | tf_op jit(solution)/shard_map/cond/branch_1_fun/ppermute | solution.py:137
  41.1 18.5 %collective-permute-start.33 = (bf16[56,2048]{1,0:T(8,128)(2,1)S(1)}, bf16[56,2048]{1,0:T(8,128)(2,1)S(1)}, u32[]{:S(2)}, u32[]{:S(2)}) collective-permute-start(bf16[56,2048]{1,0:T(8,128)(2,1)S(1)} %get-tuple-element.153), channel_id=1, source_target_pairs={{0,10},{2,8},{4,14},{6,12},{8,18},{10,16},{12,22},{14,20},{16,26},... | collective-permute-start | bytes 688136 | tf_op jit(solution)/shard_map/cond/branch_1_fun/ppermute | solution.py:137
  44.7 27.0 %collective-permute-start.34 = (bf16[56,2048]{1,0:T(8,128)(2,1)S(1)}, bf16[56,2048]{1,0:T(8,128)(2,1)S(1)}, u32[]{:S(2)}, u32[]{:S(2)}) collective-permute-start(bf16[56,2048]{1,0:T(8,128)(2,1)S(1)} %get-tuple-element.154), channel_id=1, source_target_pairs={{0,12},{2,14},{4,8},{6,10},{8,20},{10,22},{12,16},{14,18},{16,28},... | collective-permute-start | bytes 688136 | tf_op jit(solution)/shard_map/cond/branch_1_fun/ppermute | solution.py:137
  57.1 14.7 %collective-permute-start.35 = (bf16[56,2048]{1,0:T(8,128)(2,1)S(1)}, bf16[56,2048]{1,0:T(8,128)(2,1)S(1)}, u32[]{:S(2)}, u32[]{:S(2)}) collective-permute-start(bf16[56,2048]{1,0:T(8,128)(2,1)S(1)} %get-tuple-element.155), channel_id=1, source_target_pairs={{0,14},{2,12},{4,10},{6,8},{8,22},{10,20},{12,18},{14,16},{16,30},... | collective-permute-start | bytes 688136 | tf_op jit(solution)/shard_map/cond/branch_1_fun/ppermute | solution.py:137
  57.1 28.7 %collective-permute-start.37 = (bf16[56,2048]{1,0:T(8,128)(2,1)S(1)}, bf16[56,2048]{1,0:T(8,128)(2,1)S(1)}, u32[]{:S(2)}, u32[]{:S(2)}) collective-permute-start(bf16[56,2048]{1,0:T(8,128)(2,1)S(1)} %get-tuple-element.158), channel_id=1, source_target_pairs={{0,8},{2,10},{4,12},{6,14},{8,16},{10,18},{12,20},{14,22},{16,24},... | collective-permute-start | bytes 688136 | tf_op jit(solution)/shard_map/cond/branch_1_fun/ppermute | solution.py:137
  58.9 32.4 %collective-permute-start.38 = (bf16[56,2048]{1,0:T(8,128)(2,1)S(1)}, bf16[56,2048]{1,0:T(8,128)(2,1)S(1)}, u32[]{:S(2)}, u32[]{:S(2)}) collective-permute-start(bf16[56,2048]{1,0:T(8,128)(2,1)S(1)} %get-tuple-element.159), channel_id=1, source_target_pairs={{0,10},{2,8},{4,14},{6,12},{8,18},{10,16},{12,22},{14,20},{16,26},... | collective-permute-start | bytes 688136 | tf_op jit(solution)/shard_map/cond/branch_1_fun/ppermute | solution.py:137
  59.6 33.5 %collective-permute-start.39 = (bf16[56,2048]{1,0:T(8,128)(2,1)S(1)}, bf16[56,2048]{1,0:T(8,128)(2,1)S(1)}, u32[]{:S(2)}, u32[]{:S(2)}) collective-permute-start(bf16[56,2048]{1,0:T(8,128)(2,1)S(1)} %get-tuple-element.160), channel_id=1, source_target_pairs={{0,12},{2,14},{4,8},{6,10},{8,20},{10,22},{12,16},{14,18},{16,28},... | collective-permute-start | bytes 688136 | tf_op jit(solution)/shard_map/cond/branch_1_fun/ppermute | solution.py:137
  71.7 29.1 %collective-permute-start.40 = (bf16[56,2048]{1,0:T(8,128)(2,1)}, bf16[56,2048]{1,0:T(8,128)(2,1)}, u32[]{:S(2)}, u32[]{:S(2)}) collective-permute-start(bf16[56,2048]{1,0:T(8,128)(2,1)} %get-tuple-element.161), channel_id=1, source_target_pairs={{0,14},{2,12},{4,10},{6,8},{8,22},{10,20},{12,18},{14,16},{16,30},... | collective-permute-start | bytes 688136 | tf_op jit(solution)/shard_map/cond/branch_1_fun/ppermute | solution.py:137
  72.5 31.0 %collective-permute-start.22 = (bf16[56,2048]{1,0:T(8,128)(2,1)}, bf16[56,2048]{1,0:T(8,128)(2,1)S(1)}, u32[]{:S(2)}, u32[]{:S(2)}) collective-permute-start(bf16[56,2048]{1,0:T(8,128)(2,1)} %get-tuple-element.139), channel_id=1, source_target_pairs={{0,8},{2,10},{4,12},{6,14},{8,16},{10,18},{12,20},{14,22},{16,24},... | collective-permute-start | bytes 688136 | tf_op jit(solution)/shard_map/cond/branch_1_fun/ppermute | solution.py:137
  85.8 18.2 %collective-permute-start.23 = (bf16[56,2048]{1,0:T(8,128)(2,1)}, bf16[56,2048]{1,0:T(8,128)(2,1)S(1)}, u32[]{:S(2)}, u32[]{:S(2)}) collective-permute-start(bf16[56,2048]{1,0:T(8,128)(2,1)} %get-tuple-element.140), channel_id=1, source_target_pairs={{0,10},{2,8},{4,14},{6,12},{8,18},{10,16},{12,22},{14,20},{16,26},... | collective-permute-start | bytes 688136 | tf_op jit(solution)/shard_map/cond/branch_1_fun/ppermute | solution.py:137
  92.0 16.3 %collective-permute-start.24 = (bf16[56,2048]{1,0:T(8,128)(2,1)}, bf16[56,2048]{1,0:T(8,128)(2,1)S(1)}, u32[]{:S(2)}, u32[]{:S(2)}) collective-permute-start(bf16[56,2048]{1,0:T(8,128)(2,1)} %get-tuple-element.141), channel_id=1, source_target_pairs={{0,12},{2,14},{4,8},{6,10},{8,20},{10,22},{12,16},{14,18},{16,28},... | collective-permute-start | bytes 688136 | tf_op jit(solution)/shard_map/cond/branch_1_fun/ppermute | solution.py:137
  93.8 14.4 %collective-permute-start.25 = (bf16[56,2048]{1,0:T(8,128)(2,1)}, bf16[56,2048]{1,0:T(8,128)(2,1)S(1)}, u32[]{:S(2)}, u32[]{:S(2)}) collective-permute-start(bf16[56,2048]{1,0:T(8,128)(2,1)} %get-tuple-element.142), channel_id=1, source_target_pairs={{0,14},{2,12},{4,10},{6,8},{8,22},{10,20},{12,18},{14,16},{16,30},... | collective-permute-start | bytes 688136 | tf_op jit(solution)/shard_map/cond/branch_1_fun/ppermute | solution.py:137
  100.8 8.3 %collective-permute-start.31 = (bf16[128,2048]{1,0:T(8,128)(2,1)S(1)}, bf16[128,2048]{1,0:T(8,128)(2,1)S(1)}, u32[]{:S(2)}, u32[]{:S(2)}) collective-permute-start(bf16[128,2048]{1,0:T(8,128)(2,1)S(1)} %get-tuple-element.151), channel_id=1, source_target_pairs={{0,1},{1,0},{2,3},{3,2},{4,5},{5,4},{6,7},{7,6},{8,9},{9,8},{10,11... | collective-permute-start | bytes 1572872 | tf_op jit(solution)/shard_map/cond/branch_1_fun/ppermute | solution.py:549
  103.5 5.6 %collective-permute-start.41 = (bf16[128,2048]{1,0:T(8,128)(2,1)S(1)}, bf16[128,2048]{1,0:T(8,128)(2,1)S(1)}, u32[]{:S(2)}, u32[]{:S(2)}) collective-permute-start(bf16[128,2048]{1,0:T(8,128)(2,1)S(1)} %get-tuple-element.163), channel_id=1, source_target_pairs={{0,1},{1,0},{2,3},{3,2},{4,5},{5,4},{6,7},{7,6},{8,9},{9,8},{10,11... | collective-permute-start | bytes 1572872 | tf_op jit(solution)/shard_map/cond/branch_1_fun/ppermute | solution.py:549
  (10 other events, 35.9 us)

commit v2 on v1

--- a/solution.py
+++ b/solution.py
@@ -385,7 +385,7 @@
     rows = slots.shape[1]
     spare = slots.shape[2] // cycle_size - packed_rows
     full = 2 * half_width
-    tile = 512
+    tile = 1024
     steps = width // tile
 
     def kernel(*refs):

time: 115 us -> 103 us (0.90); the launches traced: 113 us -> 102 us
  starting transfers between devices: 55.5 us -> 48.7 us
  local copies, waits for them, and re-layouts: 3.06 us -> 1.43 us
  Pallas kernels: 28.5 us -> 27 us
    ppermute x16, starting transfers between devices: 44.6 us -> 37.8 us  [to_next_section(): return lax.ppermute(block, ('pp', 'cp'), route)]
    cond x12 -> x8, local copies, waits for them, and re-layouts: 2.99 us -> 1.37 us
    pallas_call x5, Pallas kernels: 9.64 us -> 8.16 us  [unpack_rows(): pl.pallas_call(kernel, in_specs=in_specs, out_specs=out_specs, scratch_sh...]
  transfers between devices with their start and end apart: 26 -> 26, of which waited for: 7 -> 7; matrix products, arithmetic and copies ran while one was open for 0% -> 0% of each run, Pallas kernels for 23% -> 24%
where the time goes in v2:
time: 103 us; the launch traced here: 102 us
  starting transfers between devices  48.7 us (47%)
  Pallas kernels  27 us (26%)
  waiting for transfers between devices  23.9 us (23%)
  local copies, waits for them, and re-layouts  1.43 us (1%)
    ppermute x16, starting transfers between devices, to_next_section(): return lax.ppermute(block, ('pp', 'cp'), route)  37.8 us
    ppermute x16, waiting for transfers between devices, to_next_section(): return lax.ppermute(block, ('pp', 'cp'), route)  17.2 us
    pallas_call x4, Pallas kernels, attend(): pl.pallas_call(kernel, in_specs=in_specs, out_specs=out_specs, out_shape=...  15.1 us
    ppermute x6, starting transfers between devices, to_partner(): return lax.ppermute(block, 'cp', [(i, i ^ mask) for i in range(size)])  10.1 us
    pallas_call x5, Pallas kernels, unpack_rows(): pl.pallas_call(kernel, in_specs=in_specs, out_specs=out_specs, scratch_sh...  8.16 us
    ppermute x6, waiting for transfers between devices, to_partner(): return lax.ppermute(block, 'cp', [(i, i ^ mask) for i in range(size)])  6.77 us
  transfers between devices with their start and end apart: 26, of which 7 were waited for; matrix products, arithmetic and copies ran while one was open for 0% of the time, Pallas kernels for 24%

profile of v2, /device:TPU:0, one launch (start us, length us, event | category | flops | bytes accessed | tf_op | source)
XLA Modules:
  0.0 102.5 jit_solution(16919878620698351101)
XLA Ops:
  1.3 5.1 %collective-permute-start.63 = (bf16[144,256]{1,0:T(8,128)(2,1)S(1)}, bf16[144,256]{1,0:T(8,128)(2,1)S(1)}, u32[]{:S(2)}, u32[]{:S(2)}) collective-permute-start(bf16[144,256]{1,0:T(8,128)(2,1)S(1)} %get-tuple-element.209.refs_3_), channel_id=1, source_target_pairs={{0,6},{2,4},{4,2},{6,0},{1,7},{3,5},{5,3},{7,1},{8,14},{10,12},{12... | collective-permute-start | bytes 221192 | tf_op jit(solution)/shard_map/ppermute | solution.py:127
  7.0 2.3 %collective-permute-start.66 = (bf16[128,768]{1,0:T(8,128)(2,1)S(1)}, bf16[128,768]{1,0:T(8,128)(2,1)S(1)}, u32[]{:S(2)}, u32[]{:S(2)}) collective-permute-start(bf16[128,768]{1,0:T(8,128)(2,1)S(1)} %get-tuple-element.211), channel_id=1, source_target_pairs={{0,4},{2,6},{4,0},{6,2},{1,5},{3,7},{5,1},{7,3},{8,12},{10,14},{12... | collective-permute-start | bytes 589832 | tf_op jit(solution)/shard_map/ppermute | solution.py:127
  9.3 2.0 %collective-permute-start.67 = (bf16[128,768]{1,0:T(8,128)(2,1)S(1)}, bf16[128,768]{1,0:T(8,128)(2,1)S(1)}, u32[]{:S(2)}, u32[]{:S(2)}) collective-permute-start(bf16[128,768]{1,0:T(8,128)(2,1)S(1)} %get-tuple-element.211), channel_id=1, source_target_pairs={{0,2},{2,0},{4,6},{6,4},{1,3},{3,1},{5,7},{7,5},{8,10},{10,8},{12,... | collective-permute-start | bytes 589832 | tf_op jit(solution)/shard_map/ppermute | solution.py:127
  12.4 5.7 %collective-permute-done.65.refs_6_ = bf16[144,256]{1,0:T(8,128)(2,1)S(1)} collective-permute-done((bf16[144,256]{1,0:T(8,128)(2,1)S(1)}, bf16[144,256]{1,0:T(8,128)(2,1)S(1)}, u32[]{:S(2)}, u32[]{:S(2)}) %collective-permute-start.65) | collective-permute-done | bytes 73760 | tf_op jit(solution)/shard_map/ppermute | solution.py:127
  18.1 5.0 %attend.19 = (s32[1]{0:T(128)}, bf16[64,2048]{1,0:T(8,128)(2,1)S(1)}, bf16[64,2048]{1,0:T(8,128)(2,1)S(1)}, bf16[64,2048]{1,0:T(8,128)(2,1)S(1)}, bf16[64,2048]{1,0:T(8,128)(2,1)S(1)}) custom-call(bf16[128,8192]{1,0:T(8,128)(2,1)} %refs_0_.1, bf16[512,256]{1,0:T(8,128)(2,1)S(1)} %get-tuple-element.207.refs_1_, ...), custom_call_target="tpu_custom_call" | custom-call | flops 20000000000 | tf_op jit(solution)/shard_map/attend/pallas_call | solution.py:370
  23.8 78.4 %conditional.1 = (bf16[128,16384]{1,0:T(8,128)(2,1)}) conditional(s32[]{:T(128)} %bitcast.5, (bf16[128,768]{1,0:T(8,128)(2,1)S(1)}, bf16[128,8192]{1,0:T(8,128)(2,1)S(1)}, bf16[512,256]{1,0:T(8,128)(2,1)S(1)}, f32[2,256,128]{2,1,0:T(8,128)S(1)}, bf16[128,768]{1,0:T(8,128)(2,1)S(1)}, /*index=5*/bf16[128,768]{1,0:T(8,128)(2,1)S(1)}, ...), branch_computations={%region_0.0_spmd, %region_1.0_spmd, %region_2.0_spmd} | conditional | bytes 51119208 | solution.py:560
  25.5 3.0 %collective-permute-start.7 = (bf16[48,2048]{1,0:T(8,128)(2,1)S(1)}, bf16[48,2048]{1,0:T(8,128)(2,1)S(1)}, u32[]{:S(2)}, u32[]{:S(2)}) collective-permute-start(bf16[48,2048]{1,0:T(8,128)(2,1)S(1)} %slice.17), channel_id=1, source_target_pairs={{0,10},{2,8},{4,14},{6,12},{8,18},{10,16},{12,22},{14,20},{16,26},... | collective-permute-start | bytes 589832 | tf_op jit(solution)/shard_map/cond/branch_0_fun/ppermute | solution.py:137
  29.8 2.2 %collective-permute-start.9 = (bf16[48,2048]{1,0:T(8,128)(2,1)S(1)}, bf16[48,2048]{1,0:T(8,128)(2,1)S(1)}, u32[]{:S(2)}, u32[]{:S(2)}) collective-permute-start(bf16[48,2048]{1,0:T(8,128)(2,1)S(1)} %slice.19), channel_id=1, source_target_pairs={{0,14},{2,12},{4,10},{6,8},{8,22},{10,20},{12,18},{14,16},{16,30},... | collective-permute-start | bytes 589832 | tf_op jit(solution)/shard_map/cond/branch_0_fun/ppermute | solution.py:137
  32.0 2.9 %attend.11 = (bf16[48,2048]{1,0:T(8,128)(2,1)S(1)}, bf16[48,2048]{1,0:T(8,128)(2,1)S(1)}, bf16[48,2048]{1,0:T(8,128)(2,1)S(1)}, bf16[48,2048]{1,0:T(8,128)(2,1)S(1)}) custom-call(bf16[128,8192]{1,0:T(8,128)(2,1)S(1)} %get-tuple-element.100.refs_0_, bf16[512,256]{1,0:T(8,128)(2,1)S(1)} %get-tuple-element.101.refs_1_, ...), custom_call_target="tpu_custom_call" | custom-call | tf_op jit(solution)/shard_map/cond/branch_0_fun/attend/pallas_call | solution.py:370
  36.4 7.7 %collective-permute-start.12 = (bf16[48,2048]{1,0:T(8,128)(2,1)S(1)}, bf16[48,2048]{1,0:T(8,128)(2,1)S(1)}, u32[]{:S(2)}, u32[]{:S(2)}) collective-permute-start(bf16[48,2048]{1,0:T(8,128)(2,1)S(1)} %get-tuple-element.120), channel_id=1, source_target_pairs={{0,10},{2,8},{4,14},{6,12},{8,18},{10,16},{12,22},{14,20},{16,26},... | collective-permute-start | bytes 589832 | tf_op jit(solution)/shard_map/cond/branch_0_fun/ppermute | solution.py:137
  44.1 3.5 %attend.12 = (bf16[48,2048]{1,0:T(8,128)(2,1)S(1)}, bf16[48,2048]{1,0:T(8,128)(2,1)S(1)}, bf16[48,2048]{1,0:T(8,128)(2,1)S(1)}, bf16[48,2048]{1,0:T(8,128)(2,1)}) custom-call(bf16[128,8192]{1,0:T(8,128)(2,1)S(1)} %get-tuple-element.100.refs_0_, bf16[512,256]{1,0:T(8,128)(2,1)S(1)} %get-tuple-element.101.refs_1_, ...), custom_call_target="tpu_custom_call" | custom-call | tf_op jit(solution)/shard_map/cond/branch_0_fun/attend/pallas_call | solution.py:370
  47.7 3.6 %collective-permute-start.13 = (bf16[48,2048]{1,0:T(8,128)(2,1)S(1)}, bf16[48,2048]{1,0:T(8,128)(2,1)S(1)}, u32[]{:S(2)}, u32[]{:S(2)}) collective-permute-start(bf16[48,2048]{1,0:T(8,128)(2,1)S(1)} %get-tuple-element.121), channel_id=1, source_target_pairs={{0,12},{2,14},{4,8},{6,10},{8,20},{10,22},{12,16},{14,18},{16,28},... | collective-permute-start | bytes 589832 | tf_op jit(solution)/shard_map/cond/branch_0_fun/ppermute | solution.py:137
  51.9 3.3 %collective-permute-start.14 = (bf16[48,2048]{1,0:T(8,128)(2,1)S(1)}, bf16[48,2048]{1,0:T(8,128)(2,1)S(1)}, u32[]{:S(2)}, u32[]{:S(2)}) collective-permute-start(bf16[48,2048]{1,0:T(8,128)(2,1)S(1)} %get-tuple-element.122), channel_id=1, source_target_pairs={{0,14},{2,12},{4,10},{6,8},{8,22},{10,20},{12,18},{14,16},{16,30},... | collective-permute-start | bytes 589832 | tf_op jit(solution)/shard_map/cond/branch_0_fun/ppermute | solution.py:137
  55.2 5.8 %collective-permute-start.17 = (bf16[48,2048]{1,0:T(8,128)(2,1)S(1)}, bf16[48,2048]{1,0:T(8,128)(2,1)S(1)}, u32[]{:S(2)}, u32[]{:S(2)}) collective-permute-start(bf16[48,2048]{1,0:T(8,128)(2,1)S(1)} %get-tuple-element.126), channel_id=1, source_target_pairs={{0,10},{2,8},{4,14},{6,12},{8,18},{10,16},{12,22},{14,20},{16,26},... | collective-permute-start | bytes 589832 | tf_op jit(solution)/shard_map/cond/branch_0_fun/ppermute | solution.py:137
  61.0 3.7 %attend.10 = (bf16[48,2048]{1,0:T(8,128)(2,1)}, bf16[48,2048]{1,0:T(8,128)(2,1)}, bf16[48,2048]{1,0:T(8,128)(2,1)}, bf16[48,2048]{1,0:T(8,128)(2,1)}) custom-call(bf16[128,8192]{1,0:T(8,128)(2,1)S(1)} %get-tuple-element.100.refs_0_, bf16[512,256]{1,0:T(8,128)(2,1)S(1)} %get-tuple-element.101.refs_1_, f32[2,256,128]{2,1,0:T(8,128)S(1)} %get-tuple-element.102.refs_2_, ...), custom_call_target="tpu_custom_call" | custom-call | tf_op jit(solution)/shard_map/cond/branch_0_fun/attend/pallas_call | solution.py:370
  64.7 7.3 %collective-permute-done.13.refs_3_ = bf16[48,2048]{1,0:T(8,128)(2,1)S(1)} collective-permute-done((bf16[48,2048]{1,0:T(8,128)(2,1)S(1)}, bf16[48,2048]{1,0:T(8,128)(2,1)S(1)}, u32[]{:S(2)}, u32[]{:S(2)}) %collective-permute-start.13) | collective-permute-done | bytes 196640 | tf_op jit(solution)/shard_map/cond/branch_0_fun/ppermute | solution.py:137
  72.0 5.6 %collective-permute-done.16.refs_1_ = bf16[48,2048]{1,0:T(8,128)(2,1)S(1)} collective-permute-done((bf16[48,2048]{1,0:T(8,128)(2,1)S(1)}, bf16[48,2048]{1,0:T(8,128)(2,1)S(1)}, u32[]{:S(2)}, u32[]{:S(2)}) %collective-permute-start.16) | collective-permute-done | bytes 196640 | tf_op jit(solution)/shard_map/cond/branch_0_fun/ppermute | solution.py:137
  77.6 2.2 %collective-permute-start.2 = (bf16[48,2048]{1,0:T(8,128)(2,1)}, bf16[48,2048]{1,0:T(8,128)(2,1)S(1)}, u32[]{:S(2)}, u32[]{:S(2)}) collective-permute-start(bf16[48,2048]{1,0:T(8,128)(2,1)} %get-tuple-element.107), channel_id=1, source_target_pairs={{0,10},{2,8},{4,14},{6,12},{8,18},{10,16},{12,22},{14,20},{16,26},... | collective-permute-start | bytes 589832 | tf_op jit(solution)/shard_map/cond/branch_0_fun/ppermute | solution.py:137
  80.5 3.5 %collective-permute-start.3 = (bf16[48,2048]{1,0:T(8,128)(2,1)}, bf16[48,2048]{1,0:T(8,128)(2,1)S(1)}, u32[]{:S(2)}, u32[]{:S(2)}) collective-permute-start(bf16[48,2048]{1,0:T(8,128)(2,1)} %get-tuple-element.108), channel_id=1, source_target_pairs={{0,12},{2,14},{4,8},{6,10},{8,20},{10,22},{12,16},{14,18},{16,28},... | collective-permute-start | bytes 589832 | tf_op jit(solution)/shard_map/cond/branch_0_fun/ppermute | solution.py:137
  85.1 2.1 %collective-permute-start.4 = (bf16[48,2048]{1,0:T(8,128)(2,1)}, bf16[48,2048]{1,0:T(8,128)(2,1)S(1)}, u32[]{:S(2)}, u32[]{:S(2)}) collective-permute-start(bf16[48,2048]{1,0:T(8,128)(2,1)} %get-tuple-element.109), channel_id=1, source_target_pairs={{0,14},{2,12},{4,10},{6,8},{8,22},{10,20},{12,18},{14,16},{16,30},... | collective-permute-start | bytes 589832 | tf_op jit(solution)/shard_map/cond/branch_0_fun/ppermute | solution.py:137
  90.2 1.8 %unpack_rows.17 = (bf16[128,16384]{1,0:T(8,128)(2,1)}, bf16[128,2048]{1,0:T(8,128)(2,1)S(1)}) custom-call(s32[3]{0:T(128)S(1)} %get-tuple-element.98.where_ref.refs_0_, bf16[48,2048]{1,0:T(8,128)(2,1)S(1)} %collective-permute-done.11.refs_1_, bf16[48,2048]{1,0:T(8,128)(2,1)S(1)} %collective-permute-done.12.refs_2_, ...), custom_call_target="tpu_custom_call", output_to_operand_aliasing={{0}: (6, {})} | custom-call | tf_op jit(solution)/shard_map/cond/branch_0_fun/unpack_rows/pallas_call | solution.py:461
  92.1 2.2 %unpack_rows.18 = (bf16[128,16384]{1,0:T(8,128)(2,1)}, bf16[128,2048]{1,0:T(8,128)(2,1)S(1)}) custom-call(s32[3]{0:T(128)S(1)} %get-tuple-element.98.where_ref.refs_0_, bf16[48,2048]{1,0:T(8,128)(2,1)S(1)} %collective-permute-done.16.refs_1_, bf16[48,2048]{1,0:T(8,128)(2,1)S(1)} %copy-done.15, ...), custom_call_target="tpu_custom_call", output_to_operand_aliasing={{0}: (6, {})} | custom-call | tf_op jit(solution)/shard_map/cond/branch_0_fun/unpack_rows/pallas_call | solution.py:461
  94.9 3.2 %collective-permute-done.3.refs_2_.refs_3_ = bf16[48,2048]{1,0:T(8,128)(2,1)S(1)} collective-permute-done((bf16[48,2048]{1,0:T(8,128)(2,1)}, bf16[48,2048]{1,0:T(8,128)(2,1)S(1)}, u32[]{:S(2)}, u32[]{:S(2)}) %collective-permute-start.3) | collective-permute-done | bytes 196640 | tf_op jit(solution)/shard_map/cond/branch_0_fun/ppermute | solution.py:137
  98.7 1.9 %unpack_rows.19.old_ref = bf16[128,16384]{1,0:T(8,128)(2,1)} custom-call(s32[3]{0:T(128)S(1)} %get-tuple-element.98.where_ref.refs_0_, bf16[48,2048]{1,0:T(8,128)(2,1)S(1)} %collective-permute-done.1.refs_0_.refs_1_, bf16[48,2048]{1,0:T(8,128)(2,1)S(1)} %collective-permute-done.2.refs_1_.refs_2_, ...), custom_call_target="tpu_custom_call", output_to_operand_aliasing={{}: (9, {})} | custom-call | tf_op jit(solution)/shard_map/cond/branch_0_fun/unpack_rows/pallas_call | solution.py:461
  (58 shorter events, 15.3 us)
Async XLA Ops:
  1.3 10.1 %collective-permute-start.63 = (bf16[144,256]{1,0:T(8,128)(2,1)S(1)}, bf16[144,256]{1,0:T(8,128)(2,1)S(1)}, u32[]{:S(2)}, u32[]{:S(2)}) collective-permute-start(bf16[144,256]{1,0:T(8,128)(2,1)S(1)} %get-tuple-element.209.refs_3_), channel_id=1, source_target_pairs={{0,6},{2,4},{4,2},{6,0},{1,7},{3,5},{5,3},{7,1},{8,14},{10,12},{12... | collective-permute-start | bytes 221192 | tf_op jit(solution)/shard_map/ppermute | solution.py:127
  6.4 6.0 %collective-permute-start.64 = (bf16[144,256]{1,0:T(8,128)(2,1)S(1)}, bf16[144,256]{1,0:T(8,128)(2,1)S(1)}, u32[]{:S(2)}, u32[]{:S(2)}) collective-permute-start(bf16[144,256]{1,0:T(8,128)(2,1)S(1)} %get-tuple-element.209.refs_3_), channel_id=1, source_target_pairs={{0,2},{2,0},{4,6},{6,4},{1,3},{3,1},{5,7},{7,5},{8,10},{10,8},{12,... | collective-permute-start | bytes 221192 | tf_op jit(solution)/shard_map/ppermute | solution.py:127
  6.4 11.7 %collective-permute-start.65 = (bf16[144,256]{1,0:T(8,128)(2,1)S(1)}, bf16[144,256]{1,0:T(8,128)(2,1)S(1)}, u32[]{:S(2)}, u32[]{:S(2)}) collective-permute-start(bf16[144,256]{1,0:T(8,128)(2,1)S(1)} %get-tuple-element.209.refs_3_), channel_id=1, source_target_pairs={{0,4},{2,6},{4,0},{6,2},{1,5},{3,7},{5,1},{7,3},{8,12},{10,14},{12... | collective-permute-start | bytes 221192 | tf_op jit(solution)/shard_map/ppermute | solution.py:127
  7.0 16.8 %collective-permute-start.66 = (bf16[128,768]{1,0:T(8,128)(2,1)S(1)}, bf16[128,768]{1,0:T(8,128)(2,1)S(1)}, u32[]{:S(2)}, u32[]{:S(2)}) collective-permute-start(bf16[128,768]{1,0:T(8,128)(2,1)S(1)} %get-tuple-element.211), channel_id=1, source_target_pairs={{0,4},{2,6},{4,0},{6,2},{1,5},{3,7},{5,1},{7,3},{8,12},{10,14},{12... | collective-permute-start | bytes 589832 | tf_op jit(solution)/shard_map/ppermute | solution.py:127
  9.3 14.5 %collective-permute-start.67 = (bf16[128,768]{1,0:T(8,128)(2,1)S(1)}, bf16[128,768]{1,0:T(8,128)(2,1)S(1)}, u32[]{:S(2)}, u32[]{:S(2)}) collective-permute-start(bf16[128,768]{1,0:T(8,128)(2,1)S(1)} %get-tuple-element.211), channel_id=1, source_target_pairs={{0,2},{2,0},{4,6},{6,4},{1,3},{3,1},{5,7},{7,5},{8,10},{10,8},{12,... | collective-permute-start | bytes 589832 | tf_op jit(solution)/shard_map/ppermute | solution.py:127
  23.9 8.1 %collective-permute-start = (bf16[128,768]{1,0:T(8,128)(2,1)S(1)}, bf16[128,768]{1,0:T(8,128)(2,1)S(1)}, u32[]{:S(2)}, u32[]{:S(2)}) collective-permute-start(bf16[128,768]{1,0:T(8,128)(2,1)S(1)} %get-tuple-element.104.refs_6_), channel_id=1, source_target_pairs={{0,2},{2,0},{4,6},{6,4},{1,3},{3,1},{5,7},{7,5},{8,10},{10,8},{12,... | collective-permute-start | bytes 589832 | tf_op jit(solution)/shard_map/cond/branch_0_fun/ppermute | solution.py:127
  24.0 12.4 %collective-permute-start.6 = (bf16[48,2048]{1,0:T(8,128)(2,1)S(1)}, bf16[48,2048]{1,0:T(8,128)(2,1)S(1)}, u32[]{:S(2)}, u32[]{:S(2)}) collective-permute-start(bf16[48,2048]{1,0:T(8,128)(2,1)S(1)} %slice.16), channel_id=1, source_target_pairs={{0,8},{2,10},{4,12},{6,14},{8,16},{10,18},{12,20},{14,22},{16,24},... | collective-permute-start | bytes 589832 | tf_op jit(solution)/shard_map/cond/branch_0_fun/ppermute | solution.py:137
  25.5 22.1 %collective-permute-start.7 = (bf16[48,2048]{1,0:T(8,128)(2,1)S(1)}, bf16[48,2048]{1,0:T(8,128)(2,1)S(1)}, u32[]{:S(2)}, u32[]{:S(2)}) collective-permute-start(bf16[48,2048]{1,0:T(8,128)(2,1)S(1)} %slice.17), channel_id=1, source_target_pairs={{0,10},{2,8},{4,14},{6,12},{8,18},{10,16},{12,22},{14,20},{16,26},... | collective-permute-start | bytes 589832 | tf_op jit(solution)/shard_map/cond/branch_0_fun/ppermute | solution.py:137
  28.5 23.3 %collective-permute-start.8 = (bf16[48,2048]{1,0:T(8,128)(2,1)S(1)}, bf16[48,2048]{1,0:T(8,128)(2,1)S(1)}, u32[]{:S(2)}, u32[]{:S(2)}) collective-permute-start(bf16[48,2048]{1,0:T(8,128)(2,1)S(1)} %slice.18), channel_id=1, source_target_pairs={{0,12},{2,14},{4,8},{6,10},{8,20},{10,22},{12,16},{14,18},{16,28},... | collective-permute-start | bytes 589832 | tf_op jit(solution)/shard_map/cond/branch_0_fun/ppermute | solution.py:137
  29.8 25.4 %collective-permute-start.9 = (bf16[48,2048]{1,0:T(8,128)(2,1)S(1)}, bf16[48,2048]{1,0:T(8,128)(2,1)S(1)}, u32[]{:S(2)}, u32[]{:S(2)}) collective-permute-start(bf16[48,2048]{1,0:T(8,128)(2,1)S(1)} %slice.19), channel_id=1, source_target_pairs={{0,14},{2,12},{4,10},{6,8},{8,22},{10,20},{12,18},{14,16},{16,30},... | collective-permute-start | bytes 589832 | tf_op jit(solution)/shard_map/cond/branch_0_fun/ppermute | solution.py:137
  34.8 20.3 %collective-permute-start.11 = (bf16[48,2048]{1,0:T(8,128)(2,1)S(1)}, bf16[48,2048]{1,0:T(8,128)(2,1)S(1)}, u32[]{:S(2)}, u32[]{:S(2)}) collective-permute-start(bf16[48,2048]{1,0:T(8,128)(2,1)S(1)} %get-tuple-element.119), channel_id=1, source_target_pairs={{0,8},{2,10},{4,12},{6,14},{8,16},{10,18},{12,20},{14,22},{16,24},... | collective-permute-start | bytes 589832 | tf_op jit(solution)/shard_map/cond/branch_0_fun/ppermute | solution.py:137
  36.4 24.6 %collective-permute-start.12 = (bf16[48,2048]{1,0:T(8,128)(2,1)S(1)}, bf16[48,2048]{1,0:T(8,128)(2,1)S(1)}, u32[]{:S(2)}, u32[]{:S(2)}) collective-permute-start(bf16[48,2048]{1,0:T(8,128)(2,1)S(1)} %get-tuple-element.120), channel_id=1, source_target_pairs={{0,10},{2,8},{4,14},{6,12},{8,18},{10,16},{12,22},{14,20},{16,26},... | collective-permute-start | bytes 589832 | tf_op jit(solution)/shard_map/cond/branch_0_fun/ppermute | solution.py:137
  47.7 24.4 %collective-permute-start.13 = (bf16[48,2048]{1,0:T(8,128)(2,1)S(1)}, bf16[48,2048]{1,0:T(8,128)(2,1)S(1)}, u32[]{:S(2)}, u32[]{:S(2)}) collective-permute-start(bf16[48,2048]{1,0:T(8,128)(2,1)S(1)} %get-tuple-element.121), channel_id=1, source_target_pairs={{0,12},{2,14},{4,8},{6,10},{8,20},{10,22},{12,16},{14,18},{16,28},... | collective-permute-start | bytes 589832 | tf_op jit(solution)/shard_map/cond/branch_0_fun/ppermute | solution.py:137
  51.9 20.2 %collective-permute-start.14 = (bf16[48,2048]{1,0:T(8,128)(2,1)S(1)}, bf16[48,2048]{1,0:T(8,128)(2,1)S(1)}, u32[]{:S(2)}, u32[]{:S(2)}) collective-permute-start(bf16[48,2048]{1,0:T(8,128)(2,1)S(1)} %get-tuple-element.122), channel_id=1, source_target_pairs={{0,14},{2,12},{4,10},{6,8},{8,22},{10,20},{12,18},{14,16},{16,30},... | collective-permute-start | bytes 589832 | tf_op jit(solution)/shard_map/cond/branch_0_fun/ppermute | solution.py:137
  55.2 22.5 %collective-permute-start.16 = (bf16[48,2048]{1,0:T(8,128)(2,1)S(1)}, bf16[48,2048]{1,0:T(8,128)(2,1)S(1)}, u32[]{:S(2)}, u32[]{:S(2)}) collective-permute-start(bf16[48,2048]{1,0:T(8,128)(2,1)S(1)} %get-tuple-element.125), channel_id=1, source_target_pairs={{0,8},{2,10},{4,12},{6,14},{8,16},{10,18},{12,20},{14,22},{16,24},... | collective-permute-start | bytes 589832 | tf_op jit(solution)/shard_map/cond/branch_0_fun/ppermute | solution.py:137
  55.2 24.7 %collective-permute-start.17 = (bf16[48,2048]{1,0:T(8,128)(2,1)S(1)}, bf16[48,2048]{1,0:T(8,128)(2,1)S(1)}, u32[]{:S(2)}, u32[]{:S(2)}) collective-permute-start(bf16[48,2048]{1,0:T(8,128)(2,1)S(1)} %get-tuple-element.126), channel_id=1, source_target_pairs={{0,10},{2,8},{4,14},{6,12},{8,18},{10,16},{12,22},{14,20},{16,26},... | collective-permute-start | bytes 589832 | tf_op jit(solution)/shard_map/cond/branch_0_fun/ppermute | solution.py:137
  61.0 23.5 %collective-permute-start.18 = (bf16[48,2048]{1,0:T(8,128)(2,1)S(1)}, bf16[48,2048]{1,0:T(8,128)(2,1)S(1)}, u32[]{:S(2)}, u32[]{:S(2)}) collective-permute-start(bf16[48,2048]{1,0:T(8,128)(2,1)S(1)} %get-tuple-element.127), channel_id=1, source_target_pairs={{0,12},{2,14},{4,8},{6,10},{8,20},{10,22},{12,16},{14,18},{16,28},... | collective-permute-start | bytes 589832 | tf_op jit(solution)/shard_map/cond/branch_0_fun/ppermute | solution.py:137
  72.0 20.0 %collective-permute-start.19 = (bf16[48,2048]{1,0:T(8,128)(2,1)}, bf16[48,2048]{1,0:T(8,128)(2,1)}, u32[]{:S(2)}, u32[]{:S(2)}) collective-permute-start(bf16[48,2048]{1,0:T(8,128)(2,1)} %get-tuple-element.128), channel_id=1, source_target_pairs={{0,14},{2,12},{4,10},{6,8},{8,22},{10,20},{12,18},{14,16},{16,30},... | collective-permute-start | bytes 589832 | tf_op jit(solution)/shard_map/cond/branch_0_fun/ppermute | solution.py:137
  72.0 22.3 %collective-permute-start.1 = (bf16[48,2048]{1,0:T(8,128)(2,1)}, bf16[48,2048]{1,0:T(8,128)(2,1)S(1)}, u32[]{:S(2)}, u32[]{:S(2)}) collective-permute-start(bf16[48,2048]{1,0:T(8,128)(2,1)} %get-tuple-element.106), channel_id=1, source_target_pairs={{0,8},{2,10},{4,12},{6,14},{8,16},{10,18},{12,20},{14,22},{16,24},... | collective-permute-start | bytes 589832 | tf_op jit(solution)/shard_map/cond/branch_0_fun/ppermute | solution.py:137
  77.6 17.2 %collective-permute-start.2 = (bf16[48,2048]{1,0:T(8,128)(2,1)}, bf16[48,2048]{1,0:T(8,128)(2,1)S(1)}, u32[]{:S(2)}, u32[]{:S(2)}) collective-permute-start(bf16[48,2048]{1,0:T(8,128)(2,1)} %get-tuple-element.107), channel_id=1, source_target_pairs={{0,10},{2,8},{4,14},{6,12},{8,18},{10,16},{12,22},{14,20},{16,26},... | collective-permute-start | bytes 589832 | tf_op jit(solution)/shard_map/cond/branch_0_fun/ppermute | solution.py:137
  80.5 17.7 %collective-permute-start.3 = (bf16[48,2048]{1,0:T(8,128)(2,1)}, bf16[48,2048]{1,0:T(8,128)(2,1)S(1)}, u32[]{:S(2)}, u32[]{:S(2)}) collective-permute-start(bf16[48,2048]{1,0:T(8,128)(2,1)} %get-tuple-element.108), channel_id=1, source_target_pairs={{0,12},{2,14},{4,8},{6,10},{8,20},{10,22},{12,16},{14,18},{16,28},... | collective-permute-start | bytes 589832 | tf_op jit(solution)/shard_map/cond/branch_0_fun/ppermute | solution.py:137
  85.1 13.0 %collective-permute-start.4 = (bf16[48,2048]{1,0:T(8,128)(2,1)}, bf16[48,2048]{1,0:T(8,128)(2,1)S(1)}, u32[]{:S(2)}, u32[]{:S(2)}) collective-permute-start(bf16[48,2048]{1,0:T(8,128)(2,1)} %get-tuple-element.109), channel_id=1, source_target_pairs={{0,14},{2,12},{4,10},{6,8},{8,22},{10,20},{12,18},{14,16},{16,30},... | collective-permute-start | bytes 589832 | tf_op jit(solution)/shard_map/cond/branch_0_fun/ppermute | solution.py:137
  92.0 6.7 %collective-permute-start.10 = (bf16[128,2048]{1,0:T(8,128)(2,1)S(1)}, bf16[128,2048]{1,0:T(8,128)(2,1)S(1)}, u32[]{:S(2)}, u32[]{:S(2)}) collective-permute-start(bf16[128,2048]{1,0:T(8,128)(2,1)S(1)} %get-tuple-element.118), channel_id=1, source_target_pairs={{0,1},{1,0},{2,3},{3,2},{4,5},{5,4},{6,7},{7,6},{8,9},{9,8},{10,11... | collective-permute-start | bytes 1572872 | tf_op jit(solution)/shard_map/cond/branch_0_fun/ppermute | solution.py:549
  94.3 4.4 %collective-permute-start.20 = (bf16[128,2048]{1,0:T(8,128)(2,1)S(1)}, bf16[128,2048]{1,0:T(8,128)(2,1)S(1)}, u32[]{:S(2)}, u32[]{:S(2)}) collective-permute-start(bf16[128,2048]{1,0:T(8,128)(2,1)S(1)} %get-tuple-element.130), channel_id=1, source_target_pairs={{0,1},{1,0},{2,3},{3,2},{4,5},{5,4},{6,7},{7,6},{8,9},{9,8},{10,11... | collective-permute-start | bytes 1572872 | tf_op jit(solution)/shard_map/cond/branch_0_fun/ppermute | solution.py:549
  (8 other events, 34.0 us)
